TPU v7x, 512 devices: a whole 4x4x16 slice. The times are simulated.
512 devices in a mesh: dom: 128 (over z, x, core), face: 4 (over y).
Axes of the slice: x: 4, y: 4, z: 16, core: 2. Of those that a mesh axis runs over, the one named last changes fastest.
Arguments:
- start: float32 [64, 65536], P(None, ('dom', 'face')), may hold values from -6 to 6
- rhs: float32 [64, 65536], P(None, ('dom', 'face')), may hold values from -6 to 6
- diag_block: bfloat16 [64, 64, 65536], P(None, None, ('dom', 'face'))
- precond: bfloat16 [64, 64, 65536], P(None, None, ('dom', 'face'))
- lift: float32 [6, 16, 64], replicated, may hold values from -0.625 to 0.625
- neighbour: int32 [6, 65536], P(None, ('dom', 'face')), may hold values from 0 to 831, as said below
- orient: int32 [6, 65536], P(None, ('dom', 'face')), may hold values from 0 to 7
- owner: int32 [65536], P(('dom', 'face')), may hold values from 0 to 127, as said below
- slot: int32 [65536], P(('dom', 'face')), may hold values from 0 to 63
Outputs:
- solution: float32 [64, 65536], P(None, ('dom', 'face'))
- coarse_op: float32 [729, 32768], P(None, ('dom', 'face'))
- coarse_rhs: float32 [27, 32768], P(None, ('dom', 'face'))
Inputs may be any that keep to these rules, and one draw needn't show every extreme that they name: neighbour of face 2 of local element e < 32 is 768 + e; of face 3 of local element 128 - 32 + j it is 800 + j; every other face f points to a face-(f xor 1) trace of a local element, below 768. Local elements 0 .. 31 of a device are owned by its own dom index, all others by another dom index; from the elements of one device at most 2 go to one owner, and some owner receives exactly 2 from each device.
All inputs are finite; a program needn't handle non-finite values.
Results may differ from a plain program's by a relative error of at most 0.0029.
Values may be sent and summed in bfloat16 or wider, within the bound.
A program may use at most 64 MiB of HBM per device.

v0:
```python
import jax
import jax.numpy as jnp
import numpy as np
from jax import lax
from jax.sharding import PartitionSpec as P

SWEEPS = 2


def with_halo(cells, sides, width):
    for axis, dim in sides:
        count = lax.axis_size(axis)
        ends = count - 1
        head = lax.slice_in_dim(cells, 0, width, axis=dim)
        tail = lax.slice_in_dim(cells, cells.shape[dim] - width, cells.shape[dim], axis=dim)
        cells = jnp.concatenate(
            [
                lax.ppermute(tail, axis, [(i, (i + 1) % count) for i in range(ends)]),
                cells,
                lax.ppermute(head, axis, [((i + 1) % count, i) for i in range(ends)]),
            ],
            axis=dim,
        )
    return cells


def turn_table():
    square = np.arange(16).reshape(4, 4)
    tables = []
    for turn in range(8):
        layout = square.T if turn & 4 else square
        if turn & 1:
            layout = layout[::-1, :]
        if turn & 2:
            layout = layout[:, ::-1]
        tables.append(layout.reshape(16))
    return np.stack(tables)


def restrict_table():
    fine_nodes = np.array([-1.0, -1.0 / np.sqrt(5.0), 1.0 / np.sqrt(5.0), 1.0])
    coarse_nodes = np.array([-1.0, 0.0, 1.0])
    basis = np.ones((4, 3))
    for column in range(3):
        for other in range(3):
            if other != column:
                basis[:, column] *= (fine_nodes - coarse_nodes[other]) / (
                    coarse_nodes[column] - coarse_nodes[other]
                )
    prolong = (
        basis[:, None, None, :, None, None]
        * basis[None, :, None, None, :, None]
        * basis[None, None, :, None, None, :]
    ).reshape(64, 27)
    return prolong.T.astype(np.float32)


def face_traces(values):
    cube = values.reshape(4, 4, 4, -1)
    planes = [cube[0], cube[3], cube[:, 0], cube[:, 3], cube[:, :, 0], cube[:, :, 3]]
    return jnp.stack([plane.reshape(16, -1) for plane in planes])


def couple(face_vals, low_in, high_in, neighbour, orient, lift):
    local_count = face_vals.shape[2]
    pool = jnp.concatenate(
        [face_vals.transpose(1, 0, 2).reshape(16, 6 * local_count), low_in, high_in], 1
    )
    picked = jnp.take(pool, neighbour.reshape(-1), axis=1).reshape(16, 6, local_count)
    tables = turn_table()
    turned = jnp.zeros_like(picked)
    for turn in range(8):
        turned = turned + jnp.where(orient[None, :, :] == turn, picked[tables[turn]], 0.0)
    return jnp.einsum("kfn,fke->ne", lift, turned, precision=lax.Precision.HIGHEST)


def galerkin(blocks, rtab):
    half = jnp.einsum(
        "cn,nms->cms",
        rtab,
        blocks,
        precision=lax.Precision.HIGHEST,
        preferred_element_type=jnp.float32,
    )
    return jnp.einsum("cms,dm->cds", half, rtab, precision=lax.Precision.HIGHEST)


def restrict(values, rtab):
    return jnp.einsum(
        "cn,ne->ce",
        rtab,
        values,
        precision=lax.Precision.HIGHEST,
        preferred_element_type=jnp.float32,
    )


def per_device(start, rhs, diag_block, precond, lift, neighbour, orient, owner, slot):
    local_count = start.shape[1]
    edge_width = local_count // 4
    staying = local_count // 4
    aggregates_here = local_count // 2
    rtab = jnp.asarray(restrict_table(), dtype=jnp.float32)

    def residual_of(values):
        face_vals = face_traces(values)
        rim_traces = jnp.concatenate(
            [face_vals[2][:, :edge_width], face_vals[3][:, local_count - edge_width :]], 1
        )
        extended = with_halo(rim_traces, (("face", 1),), edge_width)
        product = jnp.einsum(
            "nme,me->ne",
            diag_block,
            values,
            precision=lax.Precision.HIGHEST,
            preferred_element_type=jnp.float32,
        )
        coupled = couple(
            face_vals,
            extended[:, :edge_width],
            extended[:, 3 * edge_width :],
            neighbour,
            orient,
            lift,
        )
        return rhs - (product - coupled)

    solution = start
    for sweep_idx in range(SWEEPS):
        resid = residual_of(solution)
        solution = solution + jnp.einsum(
            "nme,me->ne",
            precond,
            resid,
            precision=lax.Precision.HIGHEST,
            preferred_element_type=jnp.float32,
        )
    resid = residual_of(solution)
    resid_low = lax.optimization_barrier(resid.astype(jnp.bfloat16))
    owner_count = lax.axis_size("dom")
    movers = local_count - staying
    capacity = 2 * ((movers + owner_count - 2) // (owner_count - 1))
    total_slots = owner_count * capacity
    positions = jnp.arange(local_count, dtype=jnp.int32)
    moving = positions >= staying
    hits = (
        (owner[:, None] == jnp.arange(owner_count, dtype=jnp.int32)[None, :]) & moving[:, None]
    ).astype(jnp.int32)
    earlier = jnp.cumsum(hits, 0) - hits
    rank_of = jnp.sum(earlier * hits, 1)
    target = jnp.where(moving, owner * capacity + rank_of, total_slots)
    slot_send = (
        jnp.full((1, total_slots), -1, jnp.int32).at[:, target].set(slot[None, :], mode="drop")
    )
    slot_send = slot_send.reshape(1, owner_count, capacity)
    block_send = (
        jnp.zeros((4096, total_slots), jnp.bfloat16)
        .at[:, target]
        .set(diag_block.reshape(4096, local_count), mode="drop")
        .reshape(4096, owner_count, capacity)
    )
    resid_send = (
        jnp.zeros((64, total_slots), jnp.bfloat16)
        .at[:, target]
        .set(resid_low, mode="drop")
        .reshape(64, owner_count, capacity)
    )
    blocks_in = lax.all_to_all(block_send, "dom", split_axis=1, concat_axis=1, tiled=True)
    resids_in = lax.all_to_all(resid_send, "dom", split_axis=1, concat_axis=1, tiled=True)
    slots_in = lax.all_to_all(slot_send, "dom", split_axis=1, concat_axis=1, tiled=True)
    sources = blocks_in.shape[1]
    width = blocks_in.shape[2]
    coarse_in = galerkin(blocks_in.reshape(64, 64, sources * width), rtab).reshape(
        729, sources, width
    )
    rhs_in = restrict(resids_in.reshape(64, sources * width), rtab).reshape(27, sources, width)
    stay_op = galerkin(diag_block[:, :, :staying], rtab).reshape(729, staying)
    stay_rhs = restrict(resid_low[:, :staying], rtab)
    columns_op = jnp.concatenate([coarse_in.reshape(729, total_slots), stay_op], 1)
    columns_rhs = jnp.concatenate([rhs_in.reshape(27, total_slots), stay_rhs], 1)
    slot_ids = jnp.concatenate([slots_in.reshape(total_slots), slot[:staying]])
    slot_ids = jnp.where(slot_ids < 0, aggregates_here, slot_ids)
    coarse_op = (
        jnp.zeros((729, aggregates_here), jnp.float32).at[:, slot_ids].add(columns_op, mode="drop")
    )
    coarse_rhs = (
        jnp.zeros((27, aggregates_here), jnp.float32).at[:, slot_ids].add(columns_rhs, mode="drop")
    )
    return (solution, coarse_op, coarse_rhs)


def solution(mesh):
    return jax.shard_map(
        per_device,
        mesh=mesh,
        in_specs=(
            P(None, ("dom", "face")),
            P(None, ("dom", "face")),
            P(None, None, ("dom", "face")),
            P(None, None, ("dom", "face")),
            P(),
            P(None, ("dom", "face")),
            P(None, ("dom", "face")),
            P(("dom", "face")),
            P(("dom", "face")),
        ),
        out_specs=(P(None, ("dom", "face")), P(None, ("dom", "face")), P(None, ("dom", "face"))),
        check_vma=False,
    )
```

profile of v0, /device:TPU:1, one launch (start us, length us, event | category | flops | bytes accessed | tf_op | source)
XLA Modules:
  0.0 236.3 jit_solution(1132622049801220427)
XLA Ops:
  0.6 0.7 fusion.49
  1.4 4.0 %collective-permute-start = (f32[16,32]{1,0:T(8,128)S(1)}, f32[16,32]{1,0:T(8,128)S(1)}, u32[]{:S(2)}, u32[]{:S(2)}) collective-permute-start(f32[16,32]{1,0:T(8,128)S(1)} %slice.172), channel_id=1, source_target_pairs={{0,1},{1,2},{2,3},{4,5},{5,6},{6,7},{8,9},{9,10},{10,11},{12,13},{... | collective-permute-start | bytes 6152 | tf_op jit(solution)/shard_map/ppermute | solution.py:18
  5.5 1.3 collective-permute-start.1
  6.8 0.8 fusion.31
  7.7 0.8 select_reduce_fusion
  8.5 0.7 compare_select_fusion.3
  9.2 1.1 scatter_custom_fusion
  10.3 0.8 reshape.171
  11.1 19.8 %all-to-all-start = ((s32[1,128,2]{2,0,1:T(1,128)}), s32[1,128,2]{2,0,1:T(1,128)S(1)}, u32[]{:S(2)}, u32[]{:S(2)}) async-start(s32[1,128,2]{2,0,1:T(1,128)} %bitcast.43), calls=%async_computation | async-start | bytes 131072 | tf_op jit(solution)/shard_map/all_to_all | solution.py:170
  30.9 0.7 constant_dynamic-update-slice_fusion.5
  31.6 0.8 fusion.48
  32.5 0.7 compare_select_fusion
  33.2 0.7 compare_and_fusion
  33.9 0.7 constant_dynamic-update-slice_fusion.4
  34.6 0.7 broadcast_compare_fusion.7
  35.3 0.7 pad_clamp_fusion.6
  36.0 0.7 pad_clamp_fusion
  36.7 0.7 pad_clamp_fusion.4
  37.3 0.7 pad_clamp_fusion.2
  38.0 1.6 fusion.2
  39.9 1.6 gather_fusion.24
  41.9 0.6 gather_fusion
  42.5 0.6 gather_fusion.1
  43.0 0.6 gather_fusion.7
  43.6 0.6 gather_fusion.2
  44.2 0.6 gather_fusion.3
  44.7 0.6 gather_fusion.4
  45.3 0.6 gather_fusion.5
  45.9 0.6 gather_fusion.6
  47.4 4.3 %collective-permute-start.2 = (f32[16,32]{1,0:T(8,128)S(1)}, f32[16,32]{1,0:T(8,128)S(1)}, u32[]{:S(2)}, u32[]{:S(2)}) collective-permute-start(f32[16,32]{1,0:T(8,128)S(1)} %slice.180), channel_id=1, source_target_pairs={{0,1},{1,2},{2,3},{4,5},{5,6},{6,7},{8,9},{9,10},{10,11},{12,13},{... | collective-permute-start | bytes 6152 | tf_op jit(solution)/shard_map/ppermute | solution.py:18
  51.6 1.3 collective-permute-start.3
  53.3 2.7 %collective-permute-done.3 = f32[16,32]{1,0:T(8,128)S(1)} collective-permute-done((f32[16,32]{1,0:T(8,128)S(1)}, f32[16,32]{1,0:T(8,128)S(1)}, u32[]{:S(2)}, u32[]{:S(2)}) %collective-permute-start.3) | collective-permute-done | bytes 2080 | tf_op jit(solution)/shard_map/ppermute | solution.py:20
  56.3 1.6 gather_fusion.25
  58.2 0.6 gather_fusion.8
  58.8 0.6 gather_fusion.9
  59.4 0.6 gather_fusion.10
  60.0 0.6 gather_fusion.11
  60.5 0.6 gather_fusion.12
  61.1 0.6 gather_fusion.13
  61.7 0.6 gather_fusion.14
  63.7 3.2 %collective-permute-start.4 = (f32[16,32]{1,0:T(8,128)S(1)}, f32[16,32]{1,0:T(8,128)S(1)}, u32[]{:S(2)}, u32[]{:S(2)}) collective-permute-start(f32[16,32]{1,0:T(8,128)S(1)} %slice.188), channel_id=1, source_target_pairs={{0,1},{1,2},{2,3},{4,5},{5,6},{6,7},{8,9},{9,10},{10,11},{12,13},{... | collective-permute-start | bytes 6152 | tf_op jit(solution)/shard_map/ppermute | solution.py:18
  66.9 1.3 collective-permute-start.5
  68.6 2.7 %collective-permute-done.5 = f32[16,32]{1,0:T(8,128)S(1)} collective-permute-done((f32[16,32]{1,0:T(8,128)S(1)}, f32[16,32]{1,0:T(8,128)S(1)}, u32[]{:S(2)}, u32[]{:S(2)}) %collective-permute-start.5) | collective-permute-done | bytes 2080 | tf_op jit(solution)/shard_map/ppermute | solution.py:20
  71.6 1.6 gather_fusion.26
  73.5 0.6 gather_fusion.16
  78.5 1.5 scatter_custom_fusion.3
  80.0 19.0 %all-to-all-start.2 = ((bf16[64,128,2]{0,2,1:T(2,128)(2,1)}), bf16[64,128,2]{0,2,1:T(2,128)(2,1)S(1)}, u32[]{:S(2)}, u32[]{:S(2)}) async-start(bf16[64,128,2]{0,2,1:T(2,128)(2,1)} %bitcast.67), calls=%async_computation.2 | async-start | bytes 131072 | tf_op jit(solution)/shard_map/all_to_all | solution.py:169
  99.0 1.3 copy.212
  100.3 3.4 %scatter_custom_fusion.1 = bf16[4096,256]{0,1:T(8,128)(2,1)S(1)} fusion(s32[128]{0:T(128)S(1)} %compare_select_fusion.3, bf16[4096,128]{0,1:T(8,128)(2,1)} %copy.212, bf16[]{:T(256)} %constant.46.clone.1), kind=kCustom, calls=%fused_computation.61 | custom fusion | bytes 3145730 | tf_op jit(solution)/shard_map/scatter | solution.py:159
  103.7 2.7 %reshape.173 = bf16[4096,128,2]{0,2,1:T(2,128)(2,1)} reshape(bf16[4096,256]{0,1:T(8,128)(2,1)S(1)} %scatter_custom_fusion.1) | data formatting | bytes 4194304 | tf_op jit(solution)/shard_map/reshape | solution.py:160
  106.4 7.5 %all-to-all-done.2 = bf16[64,128,2]{0,2,1:T(2,128)(2,1)S(1)} async-done(((bf16[64,128,2]{0,2,1:T(2,128)(2,1)}), bf16[64,128,2]{0,2,1:T(2,128)(2,1)S(1)}, u32[]{:S(2)}, u32[]{:S(2)}) %all-to-all-start.2) | async-done | bytes 32800 | tf_op jit(solution)/shard_map/all_to_all | solution.py:169
  113.8 8.8 %all-to-all-start.1 = ((bf16[4096,128,2]{0,2,1:T(2,128)(2,1)}), bf16[4096,128,2]{0,2,1:T(2,128)(2,1)S(1)}, u32[]{:S(2)}, u32[]{:S(2)}) async-start(bf16[4096,128,2]{0,2,1:T(2,128)(2,1)} %reshape.173), calls=%async_computation.1 | async-start | bytes 4194304 | tf_op jit(solution)/shard_map/all_to_all | solution.py:168
  122.6 1.7 copy.271
  124.3 1.4 fusion.51
  125.7 0.7 convolution_bitcast_fusion
  127.5 0.8 reduce.15
  129.0 1.8 scatter_custom_fusion.4
  130.8 0.7 copy.234
  131.5 87.1 %all-to-all-done.1 = bf16[4096,128,2]{0,2,1:T(2,128)(2,1)S(1)} async-done(((bf16[4096,128,2]{0,2,1:T(2,128)(2,1)}), bf16[4096,128,2]{0,2,1:T(2,128)(2,1)S(1)}, u32[]{:S(2)}, u32[]{:S(2)}) %all-to-all-start.1) | async-done | bytes 2097184 | tf_op jit(solution)/shard_map/all_to_all | solution.py:168
  218.5 4.1 %reshape.174 = bf16[64,64,256]{1,0,2:T(8,128)(2,1)} reshape(bf16[4096,128,2]{0,2,1:T(2,128)(2,1)S(1)} %all-to-all-done.1) | data formatting | bytes 4194304 | tf_op jit(solution)/shard_map/reshape | solution.py:173
  222.7 7.0 %copy.213 = bf16[64,64,256]{2,0,1:T(8,128)(2,1)S(1)} copy(bf16[64,64,256]{1,0,2:T(8,128)(2,1)} %reshape.174) | data formatting | bytes 4194304 | tf_op jit(solution)/shard_map/reshape | solution.py:173
  229.7 1.0 fusion.50
  230.6 2.1 fusion.7
  233.1 3.1 %scatter_custom_fusion.2 = f32[729,64]{0,1:T(8,128)} fusion(s32[288]{0:T(512)S(1)} %fusion.41, f32[729,32]{0,1:T(8,128)S(1)} %reshape.175, f32[]{:T(128)} %constant.127, f32[729,256]{0,1:T(8,128)S(1)} %copy.218, f32[]{:T(128)} %constant.34.clone.1), kind=kCustom, calls=%fused_computation.65 | custom fusion | flops 419904 | bytes 1071368 | tf_op jit(solution)/shard_map/scatter-add | solution.py:184
  (98 shorter events, 11.3 us)
Async XLA Ops:
  0.6 45.9 %copy-start = (f32[6,16,64]{2,1,0:T(8,128)S(1)}, f32[6,16,64]{2,1,0:T(8,128)}, u32[]{:S(2)}) copy-start(f32[6,16,64]{2,1,0:T(8,128)} %param.64) | copy-start | bytes 73732
  1.4 38.2 %collective-permute-start = (f32[16,32]{1,0:T(8,128)S(1)}, f32[16,32]{1,0:T(8,128)S(1)}, u32[]{:S(2)}, u32[]{:S(2)}) collective-permute-start(f32[16,32]{1,0:T(8,128)S(1)} %slice.172), channel_id=1, source_target_pairs={{0,1},{1,2},{2,3},{4,5},{5,6},{6,7},{8,9},{9,10},{10,11},{12,13},{... | collective-permute-start | bytes 6152 | tf_op jit(solution)/shard_map/ppermute | solution.py:18
  5.5 34.2 %collective-permute-start.1 = (f32[16,32]{1,0:T(8,128)S(1)}, f32[16,32]{1,0:T(8,128)S(1)}, u32[]{:S(2)}, u32[]{:S(2)}) collective-permute-start(f32[16,32]{1,0:T(8,128)S(1)} %bitcast.228), channel_id=1, source_target_pairs={{1,0},{2,1},{3,2},{5,4},{6,5},{7,6},{9,8},{10,9},{11,10},{13,12},{... | collective-permute-start | bytes 6152 | tf_op jit(solution)/shard_map/ppermute | solution.py:20
  11.1 68.9 %all-to-all-start = ((s32[1,128,2]{2,0,1:T(1,128)}), s32[1,128,2]{2,0,1:T(1,128)S(1)}, u32[]{:S(2)}, u32[]{:S(2)}) async-start(s32[1,128,2]{2,0,1:T(1,128)} %bitcast.43), calls=%async_computation | async-start | bytes 131072 | tf_op jit(solution)/shard_map/all_to_all | solution.py:170
  39.6 6.9 %copy-start.5 = (f32[64,128]{1,0:T(8,128)S(1)}, f32[64,128]{1,0:T(8,128)}, u32[]{:S(2)}) copy-start(f32[64,128]{1,0:T(8,128)} %param.61) | copy-start | bytes 98308
  39.6 7.2 %copy-start.2 = (bf16[64,64,128]{2,1,0:T(8,128)(2,1)S(1)}, bf16[64,64,128]{2,1,0:T(8,128)(2,1)}, u32[]{:S(2)}) copy-start(bf16[64,64,128]{2,1,0:T(8,128)(2,1)} %param.63) | copy-start | bytes 3145732
  41.5 5.7 %copy-start.3 = (f32[64,128]{1,0:T(8,128)S(1)}, f32[64,128]{1,0:T(8,128)}, u32[]{:S(2)}) copy-start(f32[64,128]{1,0:T(8,128)} %param.60) | copy-start | bytes 98308
  41.7 11.3 %copy-start.1 = (bf16[64,64,128]{2,1,0:T(8,128)(2,1)S(1)}, bf16[64,64,128]{2,1,0:T(8,128)(2,1)}, u32[]{:S(2)}) copy-start(bf16[64,64,128]{2,1,0:T(8,128)(2,1)} %param.62) | copy-start | bytes 3145732
  47.4 5.9 %collective-permute-start.2 = (f32[16,32]{1,0:T(8,128)S(1)}, f32[16,32]{1,0:T(8,128)S(1)}, u32[]{:S(2)}, u32[]{:S(2)}) collective-permute-start(f32[16,32]{1,0:T(8,128)S(1)} %slice.180), channel_id=1, source_target_pairs={{0,1},{1,2},{2,3},{4,5},{5,6},{6,7},{8,9},{9,10},{10,11},{12,13},{... | collective-permute-start | bytes 6152 | tf_op jit(solution)/shard_map/ppermute | solution.py:18
  51.6 4.4 %collective-permute-start.3 = (f32[16,32]{1,0:T(8,128)S(1)}, f32[16,32]{1,0:T(8,128)S(1)}, u32[]{:S(2)}, u32[]{:S(2)}) collective-permute-start(f32[16,32]{1,0:T(8,128)S(1)} %bitcast.231), channel_id=1, source_target_pairs={{1,0},{2,1},{3,2},{5,4},{6,5},{7,6},{9,8},{10,9},{11,10},{13,12},{... | collective-permute-start | bytes 6152 | tf_op jit(solution)/shard_map/ppermute | solution.py:20
  63.5 12.3 %copy-start.4 = (f32[64,128]{1,0:T(8,128)}, f32[64,128]{1,0:T(8,128)S(1)}, u32[]{:S(2)}) copy-start(f32[64,128]{1,0:T(8,128)S(1)} %bitcast_add_fusion) | copy-start | bytes 98308
  63.7 4.9 %collective-permute-start.4 = (f32[16,32]{1,0:T(8,128)S(1)}, f32[16,32]{1,0:T(8,128)S(1)}, u32[]{:S(2)}, u32[]{:S(2)}) collective-permute-start(f32[16,32]{1,0:T(8,128)S(1)} %slice.188), channel_id=1, source_target_pairs={{0,1},{1,2},{2,3},{4,5},{5,6},{6,7},{8,9},{9,10},{10,11},{12,13},{... | collective-permute-start | bytes 6152 | tf_op jit(solution)/shard_map/ppermute | solution.py:18
  66.9 4.4 %collective-permute-start.5 = (f32[16,32]{1,0:T(8,128)S(1)}, f32[16,32]{1,0:T(8,128)S(1)}, u32[]{:S(2)}, u32[]{:S(2)}) collective-permute-start(f32[16,32]{1,0:T(8,128)S(1)} %bitcast.233), channel_id=1, source_target_pairs={{1,0},{2,1},{3,2},{5,4},{6,5},{7,6},{9,8},{10,9},{11,10},{13,12},{... | collective-permute-start | bytes 6152 | tf_op jit(solution)/shard_map/ppermute | solution.py:20
  80.0 33.8 %all-to-all-start.2 = ((bf16[64,128,2]{0,2,1:T(2,128)(2,1)}), bf16[64,128,2]{0,2,1:T(2,128)(2,1)S(1)}, u32[]{:S(2)}, u32[]{:S(2)}) async-start(bf16[64,128,2]{0,2,1:T(2,128)(2,1)} %bitcast.67), calls=%async_computation.2 | async-start | bytes 131072 | tf_op jit(solution)/shard_map/all_to_all | solution.py:169
  106.4 17.9 %copy-start.6 = (f32[27,64,1]{1,0,2:T(8,128)S(1)}, f32[27,64,1]{1,0,2:T(8,128)}, u32[]{:S(2)}) copy-start(f32[27,64,1]{1,0,2:T(8,128)} %constant.123) | copy-start | bytes 20740
  113.8 104.7 %all-to-all-start.1 = ((bf16[4096,128,2]{0,2,1:T(2,128)(2,1)}), bf16[4096,128,2]{0,2,1:T(2,128)(2,1)S(1)}, u32[]{:S(2)}, u32[]{:S(2)}) async-start(bf16[4096,128,2]{0,2,1:T(2,128)(2,1)} %reshape.173), calls=%async_computation.1 | async-start | bytes 4194304 | tf_op jit(solution)/shard_map/all_to_all | solution.py:168
  124.3 2.7 %copy-start.8 = (s32[128]{0:T(128)S(1)}, s32[128]{0:T(128)}, u32[]{:S(2)}) copy-start(s32[128]{0:T(128)} %param.68) | copy-start | bytes 1540
  124.3 4.2 %copy-start.7 = (f32[27,64]{1,0:T(8,128)S(1)}, f32[27,64]{1,0:T(8,128)}, u32[]{:S(2)}) copy-start(f32[27,64]{1,0:T(8,128)} %constant.23.clone) | copy-start | bytes 20740
where the time goes:
time: 240 us; the launch traced here: 236 us
  waiting for transfers between devices  100 us (42%)
  starting transfers between devices  62.9 us (26%)
  local copies, waits for them, and re-layouts  48.7 us (20%)
  other arithmetic  16.8 us (7%)
  matrix products  6.31 us (3%)
    all_to_all x1, waiting for transfers between devices, per_device(): lax.all_to_all(block_send, 'dom', split_axis=1, concat_axis=1, tiled=True)  87.1 us
    all_to_all x1, starting transfers between devices, per_device(): lax.all_to_all(slot_send, 'dom', split_axis=1, concat_axis=1, tiled=True)  19.8 us
    all_to_all x1, starting transfers between devices, per_device(): lax.all_to_all(resid_send, 'dom', split_axis=1, concat_axis=1, tiled=True)  19 us
    gather x24, local copies, waits for them, and re-layouts, couple(): picked[tables[turn]]  13.6 us
    ppermute x3, starting transfers between devices, with_halo(): lax.ppermute(tail, axis, [(i, (i + 1) % count) for i in range(ends)])  11.5 us
    reshape x2, local copies, waits for them, and re-layouts, per_device(): blocks_in.reshape(64, 64, sources * width)  11.1 us
    all_to_all x1, starting transfers between devices, per_device(): lax.all_to_all(block_send, 'dom', split_axis=1, concat_axis=1, tiled=True)  8.79 us
    all_to_all x1, waiting for transfers between devices, per_device(): lax.all_to_all(resid_send, 'dom', split_axis=1, concat_axis=1, tiled=True)  7.45 us
  transfers between devices with their start and end apart: 9, of which 4 were waited for; matrix products, arithmetic and copies ran while one was open for 23% of the time, Pallas kernels for 0%

commit v1 on v0

v1 whole, which is shorter than its diff:
```python
import functools

import jax
import jax.numpy as jnp
import numpy as np
from jax import lax
from jax.experimental import pallas as pl
from jax.experimental.pallas import tpu as pltpu
from jax.sharding import PartitionSpec as P

SWEEPS = 2
MESH = pl.DeviceIdType.MESH
WIDTHS = (384, 256, 128)
STARTS = (0, 384, 640)
COLS = 768
SLOT_COL = 729
RHS_COL = 736
F32 = jnp.float32
BF16 = jnp.bfloat16


def line_basis():
    fine_nodes = np.array([-1.0, -1.0 / np.sqrt(5.0), 1.0 / np.sqrt(5.0), 1.0])
    coarse_nodes = np.array([-1.0, 0.0, 1.0])
    basis = np.ones((4, 3))
    for column in range(3):
        for other in range(3):
            if other != column:
                basis[:, column] *= (fine_nodes - coarse_nodes[other]) / (
                    coarse_nodes[column] - coarse_nodes[other]
                )
    return basis


def restrict_table():
    basis = line_basis()
    prolong = (
        basis[:, None, None, :, None, None]
        * basis[None, :, None, None, :, None]
        * basis[None, None, :, None, None, :]
    ).reshape(64, 27)
    return prolong.T.astype(np.float32)


def split_restrict():
    table = restrict_table()
    high = table.astype(BF16).astype(np.float32)
    both = np.zeros((64, 64), np.float32)
    both[:27] = high
    both[32:59] = table - high
    return both


def nt(lhs, rhs):
    return lax.dot_general(lhs, rhs, (((1,), (1,)), ((), ())), preferred_element_type=F32)


def mm(lhs, rhs):
    return jnp.dot(lhs, rhs, preferred_element_type=F32)


def halves(value):
    high = value.astype(BF16)
    return high, (value - high.astype(F32)).astype(BF16)


def reduce_line(v0, v1, v2, v3):
    basis = line_basis()
    outs = []
    for column in range(3):
        total = None
        for value, weight in zip((v0, v1, v2, v3), basis[:, column]):
            if weight == 0.0:
                continue
            term = value if weight == 1.0 else value * np.float32(weight)
            total = term if total is None else total + term
        outs.append(total)
    return outs


def kernel(
    nz,
    nxc,
    ny,
    start_ref,
    rhs_ref,
    diag_ref,
    prec_ref,
    lift_ref,
    nb_ref,
    ori_ref,
    own_ref,
    slot_ref,
    rmat_ref,
    sol_ref,
    op_ref,
    crhs_ref,
    line_i,
    coarse,
    val,
    trace,
    lift_t,
    index,
    turn,
    halo_out,
    halo_in,
    product,
    send_z0,
    send_z1,
    send_z2,
    recv_z0,
    recv_z1,
    recv_z2,
    send_x0,
    send_x1,
    send_x2,
    recv_x0,
    recv_x1,
    recv_x2,
    zs_sem,
    zr_sem,
    xs_sem,
    xr_sem,
    hs_sem,
    hr_sem,
):
    send_z = (send_z0, send_z1, send_z2)
    recv_z = (recv_z0, recv_z1, recv_z2)
    send_x = (send_x0, send_x1, send_x2)
    recv_x = (recv_x0, recv_x1, recv_x2)
    dom = lax.axis_index("dom")
    y = lax.axis_index("face")
    z = lax.div(dom, nxc)
    xc = lax.rem(dom, nxc)
    above = lax.rem(y + 1, ny)
    below = lax.rem(y + ny - 1, ny)
    rows = nz * nxc * 2

    barrier = pltpu.get_barrier_semaphore()

    @pl.loop(1, nz)
    def _(step):
        pl.semaphore_signal(
            barrier,
            inc=1,
            device_id=(lax.rem(z + step, nz) * nxc + xc, y),
            device_id_type=MESH,
        )

    @pl.loop(1, nxc)
    def _(step):
        pl.semaphore_signal(
            barrier,
            inc=1,
            device_id=(z * nxc + lax.rem(xc + step, nxc), y),
            device_id_type=MESH,
        )

    for other in (above, below):
        pl.semaphore_signal(barrier, inc=1, device_id=(dom, other), device_id_type=MESH)

    lane = lax.broadcasted_iota(jnp.int32, (1, 128), 1)

    coarse[pl.ds(728, 40), :] = jnp.zeros((40, 128), F32)
    rmat = rmat_ref[...]
    for rest in range(16):
        quad = []
        for i in range(4):
            both = mm(rmat, diag_ref[16 * i + rest])
            quad.append(both[:32] + both[32:])
        for out, value in enumerate(reduce_line(*quad)):
            line_i[out * 16 + rest] = value
    for a in range(3):
        planes = [[], [], []]
        for k in range(4):
            quad = [line_i[a * 16 + 4 * j + k] for j in range(4)]
            for b, value in enumerate(reduce_line(*quad)):
                planes[b].append(value)
        for b in range(3):
            for c, value in enumerate(reduce_line(*planes[b])):
                place = 27 * (9 * a + 3 * b + c)
                coarse[pl.ds(place, 27), :] = value[:27]
    coarse[pl.ds(SLOT_COL, 1), :] = slot_ref[...].astype(F32)

    own = own_ref[...]
    own_cols = jnp.broadcast_to(own, (128, 128))
    own_rows = own_cols.T
    row_id = lax.broadcasted_iota(jnp.int32, (128, 128), 0)
    col_id = lax.broadcasted_iota(jnp.int32, (128, 128), 1)
    same = (own_rows == own_cols) & (row_id >= 32) & (row_id < col_id)
    rank = jnp.sum(jnp.where(same, 1.0, 0.0), axis=0, keepdims=True)
    key = jnp.where(lane >= 32, own * 2 + rank.astype(jnp.int32), -1)
    out_rows = lax.broadcasted_iota(jnp.int32, (rows, 128), 0)
    pick = jnp.where(out_rows == key, 1.0, 0.0).astype(BF16)

    def pack(chunk):
        block = coarse[pl.ds(STARTS[chunk], WIDTHS[chunk]), :].astype(BF16)
        packed = nt(pick, block).astype(BF16)
        send_z[chunk][...] = packed.reshape(nz, nxc * 2, WIDTHS[chunk])

    pack(0)
    pack(1)

    trace[...] = jnp.zeros((128, 128), F32)
    lift_t[...] = jnp.zeros((128, 128), F32)
    for f in range(6):
        lift_t[pl.ds(f, 16, stride=8), :] = lift_ref[f]
    lift_hi, lift_lo = halves(lift_t[...].T[:64])
    index[...] = jnp.zeros((8, 128), jnp.int32)
    turn[...] = jnp.zeros((8, 128), jnp.int32)
    index[pl.ds(0, 6), :] = nb_ref[...] & 127
    turn[pl.ds(0, 6), :] = ori_ref[...]
    idx = index[...]
    flip_row = (turn[...] & 1) != 0
    flip_col = (turn[...] & 2) != 0
    swap = (turn[...] & 4) != 0
    face_id = lax.broadcasted_iota(jnp.int32, (8, 128), 0)
    lane8 = lax.broadcasted_iota(jnp.int32, (8, 128), 1)
    from_low = (face_id == 2) & (lane8 < 32)
    from_high = (face_id == 3) & (lane8 >= 96)

    def halo_copy(turn_no, side):
        other = above if side == 0 else below
        return pltpu.make_async_remote_copy(
            src_ref=halo_out.at[turn_no],
            dst_ref=halo_in.at[turn_no, side],
            send_sem=hs_sem.at[turn_no, side],
            recv_sem=hr_sem.at[turn_no, side],
            device_id=(dom, other),
            device_id_type=MESH,
        )

    def fill_halo(turn_no):
        low = jnp.concatenate([val[pl.ds(16 * i, 4), :] for i in range(4)], 0)
        high = jnp.concatenate([val[pl.ds(16 * i + 12, 4), :] for i in range(4)], 0)
        halo_out[turn_no] = jnp.where(
            lane < 64, pltpu.roll(high, 32, 1), pltpu.roll(low, 96, 1)
        )

    def matvec(matrix_ref, vector):
        for block in range(8):
            part = matrix_ref[pl.ds(8 * block, 8)].astype(F32) * vector[None]
            product[pl.ds(8 * block, 8), :] = jnp.sum(part, axis=1)
        return product[...]

    def coupled(turn_no):
        trace[pl.ds(1, 16, stride=8), :] = val[pl.ds(0, 16), :]
        trace[pl.ds(0, 16, stride=8), :] = val[pl.ds(48, 16), :]
        for i in range(4):
            trace[pl.ds(32 * i + 3, 4, stride=8), :] = val[pl.ds(16 * i, 4), :]
            trace[pl.ds(32 * i + 2, 4, stride=8), :] = val[pl.ds(16 * i + 12, 4), :]
        trace[pl.ds(5, 16, stride=8), :] = val[pl.ds(0, 16, stride=4), :]
        trace[pl.ds(4, 16, stride=8), :] = val[pl.ds(3, 16, stride=4), :]
        for side in range(2):
            halo_copy(turn_no, side).wait_recv()
        low = jnp.where(y > 0, halo_in[turn_no, 0], 0.0)
        high = jnp.where(y < ny - 1, halo_in[turn_no, 1], 0.0)
        cells = []
        for k in range(16):
            cell = jnp.take_along_axis(
                trace[pl.ds(8 * k, 8), :], idx, axis=1, mode="promise_in_bounds"
            )
            cell = jnp.where(from_low, low[k : k + 1], cell)
            cells.append(jnp.where(from_high, high[k : k + 1], cell))
        cells = [jnp.where(swap, cells[4 * (k % 4) + k // 4], cells[k]) for k in range(16)]
        cells = [jnp.where(flip_row, cells[4 * (3 - k // 4) + k % 4], cells[k]) for k in range(16)]
        cells = [jnp.where(flip_col, cells[4 * (k // 4) + 3 - k % 4], cells[k]) for k in range(16)]
        turned_hi, turned_lo = halves(jnp.concatenate(cells, 0))
        return mm(lift_hi, turned_hi) + (mm(lift_hi, turned_lo) + mm(lift_lo, turned_hi))

    val[...] = start_ref[...]
    fill_halo(0)

    pl.semaphore_wait(barrier, nz - 1 + nxc - 1 + 2)

    def send_halo(turn_no):
        for side in range(2):
            halo_copy(turn_no, side).start()

    def z_copy(chunk, other):
        return pltpu.make_async_remote_copy(
            src_ref=send_z[chunk].at[other],
            dst_ref=recv_z[chunk].at[z],
            send_sem=zs_sem.at[chunk, other],
            recv_sem=zr_sem.at[chunk, z],
            device_id=(other * nxc + xc, y),
            device_id_type=MESH,
        )

    def z_arrival(chunk, other):
        return pltpu.make_async_remote_copy(
            src_ref=send_z[chunk].at[other],
            dst_ref=recv_z[chunk].at[other],
            send_sem=zs_sem.at[chunk, other],
            recv_sem=zr_sem.at[chunk, other],
            device_id=(other * nxc + xc, y),
            device_id_type=MESH,
        )

    def x_copy(chunk, other):
        return pltpu.make_async_remote_copy(
            src_ref=send_x[chunk].at[other],
            dst_ref=recv_x[chunk].at[xc],
            send_sem=xs_sem.at[chunk, other],
            recv_sem=xr_sem.at[chunk, xc],
            device_id=(z * nxc + other, y),
            device_id_type=MESH,
        )

    def x_arrival(chunk, other):
        return pltpu.make_async_remote_copy(
            src_ref=send_x[chunk].at[other],
            dst_ref=recv_x[chunk].at[other],
            send_sem=xs_sem.at[chunk, other],
            recv_sem=xr_sem.at[chunk, other],
            device_id=(z * nxc + other, y),
            device_id_type=MESH,
        )

    def start_z(chunk):
        @pl.loop(1, nz)
        def _(step):
            far = lax.div(step, 2)
            shift = jnp.where(lax.rem(step, 2) == 1, nz // 2 - far, nz // 2 + far)
            z_copy(chunk, lax.rem(z + shift, nz)).start()

        recv_z[chunk][z] = send_z[chunk][z]

    def forward(chunk):
        @pl.loop(1, nz)
        def _(step):
            z_arrival(chunk, lax.rem(z + step, nz)).wait_recv()

        to_row = lax.broadcasted_iota(jnp.int32, (rows, rows), 0)
        from_row = lax.broadcasted_iota(jnp.int32, (rows, rows), 1)
        r = lax.rem(to_row, 2)
        src = lax.rem(lax.div(to_row, 2), nz)
        dst = lax.div(to_row, 2 * nz)
        move = jnp.where(from_row == src * (2 * nxc) + dst * 2 + r, 1.0, 0.0).astype(BF16)
        moved = mm(move, recv_z[chunk][...].reshape(rows, WIDTHS[chunk])).astype(BF16)
        send_x[chunk][...] = moved.reshape(nxc, nz * 2, WIDTHS[chunk])

        @pl.loop(1, nxc)
        def _(step):
            x_copy(chunk, lax.rem(xc + step, nxc)).start()

        recv_x[chunk][xc] = send_x[chunk][xc]

    send_halo(0)
    start_z(0)
    start_z(1)

    for sweep in range(SWEEPS):
        through = matvec(diag_ref, val[...])
        resid = rhs_ref[...] - (through - coupled(sweep))
        val[...] = val[...] + matvec(prec_ref, resid)
        fill_halo(sweep + 1)
        send_halo(sweep + 1)
    sol_ref[...] = val[...]
    through = matvec(diag_ref, val[...])
    resid = rhs_ref[...] - (through - coupled(SWEEPS))
    both = mm(rmat, resid.astype(BF16))
    coarse[pl.ds(RHS_COL, 32), :] = both[:32] + both[32:]
    pack(2)
    start_z(2)

    forward(0)
    agg_rows = lax.broadcasted_iota(jnp.int32, (64, 128), 0)
    stay = jnp.where((agg_rows == slot_ref[...]) & (lane < 32), 1.0, 0.0).astype(BF16)
    stay_hi, stay_lo = halves(coarse[...])
    staying = nt(stay, stay_hi) + nt(stay, stay_lo)
    forward(1)
    forward(2)

    for chunk in (2, 0, 1):
        @pl.loop(1, nxc)
        def _(step):
            x_arrival(chunk, lax.rem(xc + step, nxc)).wait_recv()

        table = recv_x[chunk][...].reshape(rows, WIDTHS[chunk])
        if chunk == 2:
            want = lax.broadcasted_iota(jnp.int32, (8, 128), 1) == SLOT_COL - STARTS[2]
            slots = nt(jnp.where(want, 1.0, 0.0).astype(BF16), table)[:1]
            agg = lax.broadcasted_iota(jnp.int32, (64, rows), 0)
            gather = jnp.where(agg == slots.astype(jnp.int32), 1.0, 0.0).astype(BF16)
        begin, width = STARTS[chunk], WIDTHS[chunk]
        total = mm(gather, table) + staying[:, begin : begin + width]
        if chunk == 2:
            op_ref[:, pl.ds(begin, 89)] = total[:, :89]
            place = RHS_COL - begin
            crhs_ref[...] = total.T[place : place + 27]
        else:
            op_ref[:, pl.ds(begin, width)] = total

    for chunk in range(3):
        @pl.loop(1, nz)
        def _(step):
            z_copy(chunk, lax.rem(z + step, nz)).wait_send()

        @pl.loop(1, nxc)
        def _(step):
            x_copy(chunk, lax.rem(xc + step, nxc)).wait_send()

    for turn_no in range(SWEEPS + 1):
        for side in range(2):
            halo_copy(turn_no, side).wait_send()


def per_device(sizes, start, rhs, diag_block, precond, lift, neighbour, orient, owner, slot):
    nz, nxc, ny = sizes
    vmem = pl.BlockSpec(memory_space=pltpu.VMEM)
    lift_wide = jnp.pad(lift, ((0, 0), (0, 0), (0, 64)))
    rmat = jnp.asarray(split_restrict()).astype(BF16)
    scratch = [
        pltpu.VMEM((48, 32, 128), F32),
        pltpu.VMEM((COLS, 128), F32),
        pltpu.VMEM((64, 128), F32),
        pltpu.VMEM((128, 128), F32),
        pltpu.VMEM((128, 128), F32),
        pltpu.VMEM((8, 128), jnp.int32),
        pltpu.VMEM((8, 128), jnp.int32),
        pltpu.VMEM((SWEEPS + 1, 16, 128), F32),
        pltpu.VMEM((SWEEPS + 1, 2, 16, 128), F32),
        pltpu.VMEM((64, 128), F32),
    ]
    for blocks, depth in ((nz, nxc * 2), (nz, nxc * 2), (nxc, nz * 2), (nxc, nz * 2)):
        scratch += [pltpu.VMEM((blocks, depth, width), BF16) for width in WIDTHS]
    scratch += [
        pltpu.SemaphoreType.DMA((3, nz)),
        pltpu.SemaphoreType.DMA((3, nz)),
        pltpu.SemaphoreType.DMA((3, nxc)),
        pltpu.SemaphoreType.DMA((3, nxc)),
        pltpu.SemaphoreType.DMA((SWEEPS + 1, 2)),
        pltpu.SemaphoreType.DMA((SWEEPS + 1, 2)),
    ]
    sol, op, crhs = pl.pallas_call(
        functools.partial(kernel, nz, nxc, ny),
        out_shape=(
            jax.ShapeDtypeStruct((64, 128), F32),
            jax.ShapeDtypeStruct((64, 729), F32),
            jax.ShapeDtypeStruct((27, 64), F32),
        ),
        in_specs=[vmem] * 10,
        out_specs=(vmem, vmem, vmem),
        scratch_shapes=scratch,
        compiler_params=pltpu.CompilerParams(
            collective_id=0, has_side_effects=True, vmem_limit_bytes=48 * 1024 * 1024
        ),
    )(
        start,
        rhs,
        diag_block,
        precond,
        lift_wide,
        neighbour,
        orient,
        owner.reshape(1, -1),
        slot.reshape(1, -1),
        rmat,
    )
    return (sol, op.T, crhs)


def solution(mesh):
    sizes = (mesh.shape["dom"] // 8, 8, mesh.shape["face"])
    return jax.shard_map(
        functools.partial(per_device, sizes),
        mesh=mesh,
        in_specs=(
            P(None, ("dom", "face")),
            P(None, ("dom", "face")),
            P(None, None, ("dom", "face")),
            P(None, None, ("dom", "face")),
            P(),
            P(None, ("dom", "face")),
            P(None, ("dom", "face")),
            P(("dom", "face")),
            P(("dom", "face")),
        ),
        out_specs=(P(None, ("dom", "face")), P(None, ("dom", "face")), P(None, ("dom", "face"))),
        check_vma=False,
    )
```

time: 240 us -> 49.9 us (0.21); the launches traced: 236 us -> 49.7 us
  waiting for transfers between devices: 100 us -> 0 us
  starting transfers between devices: 62.9 us -> 0 us
  Pallas kernels: 0 us -> 43.7 us
  local copies, waits for them, and re-layouts: 48.7 us -> 5.22 us
  other arithmetic: 16.8 us -> 0 us
  matrix products: 6.31 us -> 0 us
    all_to_all x3 -> x0, waiting for transfers between devices: 94.5 us -> none  [the longest x1 87.1 us: per_device(): lax.all_to_all(block_send, 'dom', split_axis=1, concat_axis=1, tiled=True)]
    all_to_all x3 -> x0, starting transfers between devices: 47.6 us -> none  [the longest x1 19.8 us: per_device(): lax.all_to_all(slot_send, 'dom', split_axis=1, concat_axis=1, tiled=True)]
    pallas_call x0 -> x1, Pallas kernels: none -> 43.7 us  [per_device(): pl.pallas_call(functools.partial(kernel, nz, nxc, ny), out_shape=(jax.Sha...]
    gather x27 -> x0, local copies, waits for them, and re-layouts: 18.3 us -> none  [the longest x24 13.6 us: couple(): picked[tables[turn]]]
    reshape x12 -> x0, local copies, waits for them, and re-layouts: 16.6 us -> none  [the longest x2 11.1 us: per_device(): blocks_in.reshape(64, 64, sources * width)]
    ppermute x6 -> x0, starting transfers between devices: 15.3 us -> none  [the longest x3 11.5 us: with_halo(): lax.ppermute(tail, axis, [(i, (i + 1) % count) for i in range(ends)])]
    dot_general x9 -> x0, matrix products: 6.31 us -> none  [the longest x2 2.84 us: galerkin(): jnp.einsum('cms,dm->cds', half, rtab, precision=lax.Precision.HIGHEST)]
    scatter x3 -> x0, local copies, waits for them, and re-layouts: 5.99 us -> none  [the longest x1 3.42 us: per_device(): block_send = jnp.zeros((4096, total_slots), jnp.bfloat16).at[:, target].s...]
  transfers between devices with their start and end apart: 9 -> 0, of which waited for: 4 -> 0; matrix products, arithmetic and copies ran while one was open for 23% -> 0% of each run, Pallas kernels for 0% -> 0%
where the time goes in v1:
time: 49.9 us; the launch traced here: 49.7 us
  Pallas kernels  43.7 us (88%)
  local copies, waits for them, and re-layouts  5.22 us (10%)
  between operations  0.76 us (2%)
    pallas_call x1, Pallas kernels, per_device(): pl.pallas_call(functools.partial(kernel, nz, nxc, ny), out_shape=(jax.Sha...  43.7 us
    unnamed x21, local copies, waits for them, and re-layouts  4.37 us

profile of v1, /device:TPU:1, one launch (start us, length us, event | category | flops | bytes accessed | tf_op | source)
XLA Modules:
  0.0 49.7 jit_solution(13464078505238088678)
XLA Ops:
  0.6 0.0 copy-start.2
  0.6 0.0 copy-start.3
  0.7 0.0 copy-start.4
  0.7 0.0 copy-start.5
  0.7 0.0 copy-start.6
  0.7 0.0 copy-start.7
  0.7 0.0 copy-start.8
  0.7 0.8 %pad.4.lift_ref = f32[6,16,128]{2,1,0:T(8,128)S(1)} pad(f32[6,16,64]{2,1,0:T(8,128)} %param.14, f32[]{:T(128)} %constant.4.clone.1), padding=0_0x0_0x0_64 | pad | bytes 73732 | tf_op jit(solution)/shard_map/jit(_pad)/pad | solution.py:412
  1.5 0.0 copy-done.2
  1.6 0.0 copy-done.3
  1.6 0.0 copy-done.4
  1.6 0.0 copy-done.5
  1.6 0.0 copy-done.6
  1.6 0.0 copy-done.7
  1.6 0.0 copy-done.8
  1.6 0.0 copy-start
  1.6 1.2 %copy-done = bf16[64,64,128]{2,1,0:T(8,128)(2,1)S(1)} copy-done((bf16[64,64,128]{2,1,0:T(8,128)(2,1)S(1)}, bf16[64,64,128]{2,1,0:T(8,128)(2,1)}, u32[]{:S(2)}) %copy-start) | copy-done | bytes 1048600
  2.8 0.0 copy-start.1
  2.8 1.2 %copy-done.1 = bf16[64,64,128]{2,1,0:T(8,128)(2,1)S(1)} copy-done((bf16[64,64,128]{2,1,0:T(8,128)(2,1)S(1)}, bf16[64,64,128]{2,1,0:T(8,128)(2,1)}, u32[]{:S(2)}) %copy-start.1) | copy-done | bytes 1048600
  4.1 43.7 %shard_map.121 = (f32[64,128]{1,0:T(8,128)S(1)}, f32[64,729]{1,0:T(8,128)S(1)}, f32[27,64]{1,0:T(8,128)S(1)}) custom-call(f32[64,128]{1,0:T(8,128)S(1)} %copy-done.2, f32[64,128]{1,0:T(8,128)S(1)} %copy-done.3, bf16[64,64,128]{2,1,0:T(8,128)(2,1)S(1)} %copy-done, bf16[64,64,128]{2,1,0:T(8,128)(2,1)S(1)} %copy-done.1, f32[6,16,128]{2,1,0:T(8,128)S(1)} %pad.4.lift_ref, ...), custom_call_target="tpu_custom_call" | custom-call | tf_op jit(solution)/shard_map/pallas_call | solution.py:436
  47.8 0.6 %copy.16 = f32[64,128]{1,0:T(8,128)} copy(f32[64,128]{1,0:T(8,128)S(1)} %get-tuple-element.12) | data formatting | bytes 65536
  48.4 0.7 %copy.17 = f32[729,64]{0,1:T(8,128)} copy(f32[729,64]{0,1:T(8,128)S(1)} %bitcast.3) | data formatting | bytes 373248
  49.0 0.6 %copy.18 = f32[27,64]{1,0:T(8,128)} copy(f32[27,64]{1,0:T(8,128)S(1)} %get-tuple-element.14) | data formatting | bytes 13824
Async XLA Ops:
  0.6 0.9 %copy-start.2 = (f32[64,128]{1,0:T(8,128)S(1)}, f32[64,128]{1,0:T(8,128)}, u32[]{:S(2)}) copy-start(f32[64,128]{1,0:T(8,128)} %start_ref.1) | copy-start | bytes 98308
  0.6 0.9 %copy-start.3 = (f32[64,128]{1,0:T(8,128)S(1)}, f32[64,128]{1,0:T(8,128)}, u32[]{:S(2)}) copy-start(f32[64,128]{1,0:T(8,128)} %rhs_ref.1) | copy-start | bytes 98308
  0.7 0.9 %copy-start.4 = (bf16[64,64]{1,0:T(8,128)(2,1)S(1)}, bf16[64,64]{1,0:T(8,128)(2,1)}, u32[]{:S(2)}) copy-start(bf16[64,64]{1,0:T(8,128)(2,1)} %constant.16.rmat_ref) | copy-start | bytes 24580
  0.7 0.9 %copy-start.5 = (s32[6,128]{1,0:T(8,128)S(1)}, s32[6,128]{1,0:T(8,128)}, u32[]{:S(2)}) copy-start(s32[6,128]{1,0:T(8,128)} %nb_ref.1) | copy-start | bytes 9220
  0.7 0.9 %copy-start.6 = (s32[6,128]{1,0:T(8,128)S(1)}, s32[6,128]{1,0:T(8,128)}, u32[]{:S(2)}) copy-start(s32[6,128]{1,0:T(8,128)} %ori_ref.1) | copy-start | bytes 9220
  0.7 0.9 %copy-start.7 = (s32[128]{0:T(128)S(1)}, s32[128]{0:T(128)}, u32[]{:S(2)}) copy-start(s32[128]{0:T(128)} %param.17) | copy-start | bytes 1540
  0.7 0.9 %copy-start.8 = (s32[128]{0:T(128)S(1)}, s32[128]{0:T(128)}, u32[]{:S(2)}) copy-start(s32[128]{0:T(128)} %param.18) | copy-start | bytes 1540
  1.6 1.2 %copy-start = (bf16[64,64,128]{2,1,0:T(8,128)(2,1)S(1)}, bf16[64,64,128]{2,1,0:T(8,128)(2,1)}, u32[]{:S(2)}) copy-start(bf16[64,64,128]{2,1,0:T(8,128)(2,1)} %diag_ref.1) | copy-start | bytes 3145732
  2.8 1.2 %copy-start.1 = (bf16[64,64,128]{2,1,0:T(8,128)(2,1)S(1)}, bf16[64,64,128]{2,1,0:T(8,128)(2,1)}, u32[]{:S(2)}) copy-start(bf16[64,64,128]{2,1,0:T(8,128)(2,1)} %prec_ref.1) | copy-start | bytes 3145732

commit v2 on v1

v2 whole, which is shorter than its diff:
```python
import functools

import jax
import jax.numpy as jnp
import numpy as np
from jax import lax
from jax.experimental import pallas as pl
from jax.experimental.pallas import tpu as pltpu
from jax.sharding import PartitionSpec as P

SWEEPS = 2
MESH = pl.DeviceIdType.MESH
WIDTHS = (384, 256, 128)
STARTS = (0, 384, 640)
COLS = 768
SLOT_COL = 383
RHS_COL = 736
F32 = jnp.float32
BF16 = jnp.bfloat16


def line_basis():
    fine_nodes = np.array([-1.0, -1.0 / np.sqrt(5.0), 1.0 / np.sqrt(5.0), 1.0])
    coarse_nodes = np.array([-1.0, 0.0, 1.0])
    basis = np.ones((4, 3))
    for column in range(3):
        for other in range(3):
            if other != column:
                basis[:, column] *= (fine_nodes - coarse_nodes[other]) / (
                    coarse_nodes[column] - coarse_nodes[other]
                )
    return basis


def restrict_table():
    basis = line_basis()
    prolong = (
        basis[:, None, None, :, None, None]
        * basis[None, :, None, None, :, None]
        * basis[None, None, :, None, None, :]
    ).reshape(64, 27)
    return prolong.T.astype(np.float32)


def split_restrict():
    table = restrict_table()
    high = table.astype(BF16).astype(np.float32)
    both = np.zeros((64, 64), np.float32)
    both[:27] = high
    both[32:59] = table - high
    return both


def nt(lhs, rhs):
    return lax.dot_general(lhs, rhs, (((1,), (1,)), ((), ())), preferred_element_type=F32)


def mm(lhs, rhs):
    return jnp.dot(lhs, rhs, preferred_element_type=F32)


def halves(value):
    high = value.astype(BF16)
    return high, (value - high.astype(F32)).astype(BF16)


def reduce_line(v0, v1, v2, v3):
    basis = line_basis()
    outs = []
    for column in range(3):
        total = None
        for value, weight in zip((v0, v1, v2, v3), basis[:, column]):
            if weight == 0.0:
                continue
            term = value if weight == 1.0 else value * np.float32(weight)
            total = term if total is None else total + term
        outs.append(total)
    return outs


def one_hot(mask):
    return jnp.where(mask, 1.0, 0.0).astype(BF16)


def kernel(
    nz,
    nxc,
    ny,
    start_hbm,
    rhs_hbm,
    diag_hbm,
    prec_hbm,
    lift_hbm,
    nb_hbm,
    ori_hbm,
    own_hbm,
    slot_hbm,
    rmat_hbm,
    sol_ref,
    op_ref,
    crhs_ref,
    val,
    rhs_ref,
    diag_ref,
    prec_ref,
    lift_ref,
    nb_ref,
    ori_ref,
    own_ref,
    slot_ref,
    rmat_ref,
    line,
    coarse,
    trace,
    lift_t,
    index,
    turn,
    halo_out,
    halo_in,
    product,
    pick_x,
    move_zx,
    move_xz,
    send_z0,
    send_z1,
    send_z2,
    recv_z0,
    recv_z1,
    recv_z2,
    send_x0,
    send_x1,
    send_x2,
    recv_x0,
    recv_x1,
    recv_x2,
    in_sem,
    zs_sem,
    zr_sem,
    xs_sem,
    xr_sem,
    hs_sem,
    hr_sem,
    near_sem,
    far_sem,
):
    send_z = (send_z0, send_z1, send_z2)
    recv_z = (recv_z0, recv_z1, recv_z2)
    send_x = (send_x0, send_x1, send_x2)
    recv_x = (recv_x0, recv_x1, recv_x2)
    dom = lax.axis_index("dom")
    y = lax.axis_index("face")
    z = lax.div(dom, nxc)
    xc = lax.rem(dom, nxc)
    above = lax.rem(y + 1, ny)
    below = lax.rem(y + ny - 1, ny)
    rows = nz * nxc * 2

    def at_z(shift):
        return (lax.rem(z + shift + nz, nz) * nxc + xc, y)

    barrier = pltpu.get_barrier_semaphore()
    for other in (above, below):
        pl.semaphore_signal(barrier, inc=1, device_id=(dom, other), device_id_type=MESH)
    for shift in (1, -1, 2, -2):
        pl.semaphore_signal(barrier, inc=1, device_id=at_z(shift), device_id_type=MESH)

    @pl.loop(1, nxc)
    def _(step):
        pl.semaphore_signal(
            barrier,
            inc=1,
            device_id=(z * nxc + lax.rem(xc + step, nxc), y),
            device_id_type=MESH,
        )

    pairs = [
        (start_hbm, val),
        (rmat_hbm, rmat_ref),
        (own_hbm, own_ref),
        (slot_hbm, slot_ref),
        (nb_hbm, nb_ref),
        (ori_hbm, ori_ref),
        (lift_hbm, lift_ref),
        (rhs_hbm, rhs_ref),
        (prec_hbm, prec_ref),
    ]
    fetches = [
        pltpu.make_async_copy(src, dst, in_sem.at[place])
        for place, (src, dst) in enumerate(pairs)
    ]
    slabs = [
        pltpu.make_async_copy(
            diag_hbm.at[pl.ds(16 * i, 16)], diag_ref.at[pl.ds(16 * i, 16)], in_sem.at[9 + i]
        )
        for i in range(4)
    ]
    for fetch in fetches[:4] + slabs + fetches[4:]:
        fetch.start()

    lane = lax.broadcasted_iota(jnp.int32, (1, 128), 1)

    def halo_copy(turn_no, side):
        return pltpu.make_async_remote_copy(
            src_ref=halo_out.at[turn_no, side],
            dst_ref=halo_in.at[turn_no, side],
            send_sem=hs_sem.at[turn_no],
            recv_sem=hr_sem.at[turn_no],
            device_id=(dom, above if side == 0 else below),
            device_id_type=MESH,
        )

    def halo_both(turn_no):
        return pltpu.make_async_remote_copy(
            src_ref=halo_out.at[turn_no],
            dst_ref=halo_in.at[turn_no],
            send_sem=hs_sem.at[turn_no],
            recv_sem=hr_sem.at[turn_no],
            device_id=(dom, above),
            device_id_type=MESH,
        )

    def send_halo(turn_no):
        low = jnp.concatenate([val[pl.ds(16 * i, 4), :] for i in range(4)], 0)
        high = jnp.concatenate([val[pl.ds(16 * i + 12, 4), :] for i in range(4)], 0)
        halo_out[turn_no, 0] = pltpu.roll(high, 32, 1)
        halo_out[turn_no, 1] = pltpu.roll(low, 96, 1)

    fetches[0].wait()
    send_halo(0)

    pl.semaphore_wait(barrier, 2 + 4 + nxc - 1)
    for side in range(2):
        halo_copy(0, side).start()
    if nz > 4:
        for side, shift in enumerate((2, -2)):
            pl.semaphore_signal(
                near_sem.at[side], inc=1, device_id=at_z(shift), device_id_type=MESH
            )

    coarse[pl.ds(728, 40), :] = jnp.zeros((40, 128), F32)
    for fetch in fetches[1:4]:
        fetch.wait()
    rmat = rmat_ref[...]
    for i in range(4):
        slabs[i].wait()
        planes = [[], [], []]
        for j in range(4):
            quad = []
            for k in range(4):
                both = mm(rmat, diag_ref[16 * i + 4 * j + k])
                quad.append(both[:32] + both[32:])
            for c, value in enumerate(reduce_line(*quad)):
                planes[c].append(value)
        for c in range(3):
            for b, value in enumerate(reduce_line(*planes[c])):
                line[9 * i + 3 * b + c] = value
    for bc in range(9):
        for a, value in enumerate(reduce_line(*[line[9 * i + bc] for i in range(4)])):
            place = 27 * (9 * a + bc)
            if place > SLOT_COL:
                coarse[pl.ds(place + 1, 27), :] = value[:27]
            elif place + 27 <= SLOT_COL:
                coarse[pl.ds(place, 27), :] = value[:27]
            else:
                head = SLOT_COL - place
                coarse[pl.ds(place, head), :] = value[:head]
                coarse[pl.ds(SLOT_COL + 1, 27 - head), :] = value[head:27]
    coarse[pl.ds(SLOT_COL, 1), :] = slot_ref[...].astype(F32)

    own = own_ref[...]
    own_cols = jnp.broadcast_to(own, (128, 128))
    own_rows = own_cols.T
    row_id = lax.broadcasted_iota(jnp.int32, (128, 128), 0)
    col_id = lax.broadcasted_iota(jnp.int32, (128, 128), 1)
    same = (own_rows == own_cols) & (row_id >= 32) & (row_id < col_id)
    rank = jnp.sum(jnp.where(same, 1.0, 0.0), axis=0, keepdims=True)
    key = jnp.where(lane >= 32, own * 2 + rank.astype(jnp.int32), -1)
    out_rows = lax.broadcasted_iota(jnp.int32, (rows, 128), 0)
    pick_z = one_hot(out_rows == key)

    def columns(chunk):
        return coarse[pl.ds(STARTS[chunk], WIDTHS[chunk]), :].astype(BF16)

    for chunk in (0, 1):
        packed = nt(pick_z, columns(chunk)).astype(BF16)
        send_z[chunk][...] = packed.reshape(nz, nxc * 2, WIDTHS[chunk])

    def z_copy(chunk, shift):
        other = lax.rem(z + shift + nz, nz)
        return pltpu.make_async_remote_copy(
            src_ref=send_z[chunk].at[other],
            dst_ref=recv_z[chunk].at[z],
            send_sem=zs_sem.at[chunk],
            recv_sem=zr_sem.at[chunk],
            device_id=(other * nxc + xc, y),
            device_id_type=MESH,
        )

    def z_all(chunk):
        return pltpu.make_async_remote_copy(
            src_ref=send_z[chunk].at[pl.ds(0, nz - 1)],
            dst_ref=recv_z[chunk].at[pl.ds(0, nz - 1)],
            send_sem=zs_sem.at[chunk],
            recv_sem=zr_sem.at[chunk],
            device_id=at_z(1),
            device_id_type=MESH,
        )

    def x_copy(chunk, step):
        other = lax.rem(xc + step, nxc)
        return pltpu.make_async_remote_copy(
            src_ref=send_x[chunk].at[other],
            dst_ref=recv_x[chunk].at[xc],
            send_sem=xs_sem.at[chunk],
            recv_sem=xr_sem.at[chunk],
            device_id=(z * nxc + other, y),
            device_id_type=MESH,
        )

    def x_all(chunk):
        return pltpu.make_async_remote_copy(
            src_ref=send_x[chunk].at[pl.ds(0, nxc - 1)],
            dst_ref=recv_x[chunk].at[pl.ds(0, nxc - 1)],
            send_sem=xs_sem.at[chunk],
            recv_sem=xr_sem.at[chunk],
            device_id=(z * nxc + lax.rem(xc + 1, nxc), y),
            device_id_type=MESH,
        )

    def z_pair(chunk, shift):
        z_copy(chunk, shift).start()
        if 2 * shift != nz:
            z_copy(chunk, -shift).start()

    def start_x(chunk):
        @pl.loop(1, nxc)
        def _(step):
            x_copy(chunk, step).start()

        recv_x[chunk][xc] = send_x[chunk][xc]

    half = nz // 2
    for chunk in (0, 1):
        for shift in range(1, min(2, half) + 1):
            z_pair(chunk, shift)
    if nz > 4:
        for side in range(2):
            pl.semaphore_wait(near_sem.at[side], 1)
        if nz > 8:
            for side, shift in enumerate((4, -4)):
                pl.semaphore_signal(
                    far_sem.at[side], inc=1, device_id=at_z(shift), device_id_type=MESH
                )
        for chunk in (0, 1):
            for shift in range(3, min(4, half) + 1):
                z_pair(chunk, shift)
    for chunk in (0, 1):
        recv_z[chunk][z] = send_z[chunk][z]

    for fetch in fetches[4:7]:
        fetch.wait()
    trace[...] = jnp.zeros((128, 128), F32)
    lift_t[...] = jnp.zeros((128, 128), F32)
    for f in range(6):
        lift_t[pl.ds(f, 16, stride=8), :] = jnp.concatenate(
            [lift_ref[f], jnp.zeros((16, 64), F32)], 1
        )
    lift_hi, lift_lo = halves(lift_t[...].T[:64])
    index[...] = jnp.zeros((8, 128), jnp.int32)
    turn[...] = jnp.zeros((8, 128), jnp.int32)
    index[pl.ds(0, 6), :] = nb_ref[...] & 127
    turn[pl.ds(0, 6), :] = ori_ref[...]
    idx = index[...]
    flip_row = (turn[...] & 1) != 0
    flip_col = (turn[...] & 2) != 0
    swap = (turn[...] & 4) != 0
    face_id = lax.broadcasted_iota(jnp.int32, (8, 128), 0)
    lane8 = lax.broadcasted_iota(jnp.int32, (8, 128), 1)
    from_low = (face_id == 2) & (lane8 < 32)
    from_high = (face_id == 3) & (lane8 >= 96)

    def matvec(matrix_ref, vector):
        for block in range(8):
            part = matrix_ref[pl.ds(8 * block, 8)].astype(F32) * vector[None]
            product[pl.ds(8 * block, 8), :] = jnp.sum(part, axis=1)
        return product[...]

    def coupled(turn_no):
        trace[pl.ds(1, 16, stride=8), :] = val[pl.ds(0, 16), :]
        trace[pl.ds(0, 16, stride=8), :] = val[pl.ds(48, 16), :]
        for i in range(4):
            trace[pl.ds(32 * i + 3, 4, stride=8), :] = val[pl.ds(16 * i, 4), :]
            trace[pl.ds(32 * i + 2, 4, stride=8), :] = val[pl.ds(16 * i + 12, 4), :]
        trace[pl.ds(5, 16, stride=8), :] = val[pl.ds(0, 16, stride=4), :]
        trace[pl.ds(4, 16, stride=8), :] = val[pl.ds(3, 16, stride=4), :]
        cells = [
            jnp.take_along_axis(
                trace[pl.ds(8 * k, 8), :], idx, axis=1, mode="promise_in_bounds"
            )
            for k in range(16)
        ]
        halo_both(turn_no).wait_recv()
        low = jnp.where(y > 0, halo_in[turn_no, 0], 0.0)
        high = jnp.where(y < ny - 1, halo_in[turn_no, 1], 0.0)
        cells = [jnp.where(from_low, low[k : k + 1], cells[k]) for k in range(16)]
        cells = [jnp.where(from_high, high[k : k + 1], cells[k]) for k in range(16)]
        cells = [jnp.where(swap, cells[4 * (k % 4) + k // 4], cells[k]) for k in range(16)]
        cells = [jnp.where(flip_row, cells[4 * (3 - k // 4) + k % 4], cells[k]) for k in range(16)]
        cells = [jnp.where(flip_col, cells[4 * (k // 4) + 3 - k % 4], cells[k]) for k in range(16)]
        turned_hi, turned_lo = halves(jnp.concatenate(cells, 0))
        return mm(lift_hi, turned_hi) + (mm(lift_hi, turned_lo) + mm(lift_lo, turned_hi))

    fetches[7].wait()
    for sweep in range(SWEEPS):
        through = rhs_ref[...] - matvec(diag_ref, val[...])
        resid = through + coupled(sweep)
        if sweep == 0:
            fetches[8].wait()
        val[...] = val[...] + matvec(prec_ref, resid)
        send_halo(sweep + 1)
        for side in range(2):
            halo_copy(sweep + 1, side).start()
        if sweep == 0:
            if nz > 8:
                for side in range(2):
                    pl.semaphore_wait(far_sem.at[side], 1)
                for chunk in (0, 1):
                    for shift in range(half, 4, -1):
                        z_pair(chunk, shift)
            s = lax.broadcasted_iota(jnp.int32, (rows, 128), 0)
            deep = 2 * nz
            wide = 2 * nxc
            target = (((s & (deep - 1)) >> 1) * wide) + ((s // deep) * 2) + (s & 1)
            pick_x[...] = one_hot(target == key)
            s = lax.broadcasted_iota(jnp.int32, (rows, rows), 0)
            q = lax.broadcasted_iota(jnp.int32, (rows, rows), 1)
            target = (((s & (deep - 1)) >> 1) * wide) + ((s // deep) * 2) + (s & 1)
            move_zx[...] = one_hot(q == target)
            target = (((s & (wide - 1)) >> 1) * deep) + ((s // wide) * 2) + (s & 1)
            move_xz[...] = one_hot(q == target)
    sol_ref[...] = val[...]
    through = rhs_ref[...] - matvec(diag_ref, val[...])
    resid = through + coupled(SWEEPS)
    both = mm(rmat, resid.astype(BF16))
    coarse[pl.ds(RHS_COL, 32), :] = both[:32] + both[32:]
    packed = nt(pick_x[...], columns(2)).astype(BF16)
    send_x[2][...] = packed.reshape(nxc, nz * 2, WIDTHS[2])
    start_x(2)

    def forward(chunk):
        z_all(chunk).wait_recv()
        table = recv_z[chunk][...].reshape(rows, WIDTHS[chunk])
        moved = mm(move_zx[...], table).astype(BF16)
        send_x[chunk][...] = moved.reshape(nxc, nz * 2, WIDTHS[chunk])
        start_x(chunk)

    forward(0)
    agg_rows = lax.broadcasted_iota(jnp.int32, (64, 128), 0)
    stay = one_hot((agg_rows == slot_ref[...]) & (lane < 32))
    stay_hi, stay_lo = halves(coarse[...])
    staying = nt(stay, stay_hi) + nt(stay, stay_lo)

    x_all(2).wait_recv()
    moved = mm(move_xz[...], recv_x[2][...].reshape(rows, WIDTHS[2])).astype(BF16)
    send_z[2][...] = moved.reshape(nz, nxc * 2, WIDTHS[2])
    for shift in range(half, 0, -1):
        z_pair(2, shift)
    recv_z[2][z] = send_z[2][z]

    forward(1)
    x_all(0).wait_recv()
    table = recv_x[0][...].reshape(rows, WIDTHS[0])
    want = lax.broadcasted_iota(jnp.int32, (8, WIDTHS[0]), 1) == SLOT_COL
    slots = nt(one_hot(want), table)[:1]
    agg = lax.broadcasted_iota(jnp.int32, (64, rows), 0)
    gather = one_hot(agg == slots.astype(jnp.int32))
    gather_zx = mm(gather, move_zx[...]).astype(BF16)
    total = mm(gather, table) + staying[:, : WIDTHS[0]]
    op_ref[:, pl.ds(0, SLOT_COL)] = total[:, :SLOT_COL]
    x_all(1).wait_recv()
    table = recv_x[1][...].reshape(rows, WIDTHS[1])
    total = mm(gather, table) + staying[:, STARTS[1] : STARTS[2]]
    op_ref[:, pl.ds(SLOT_COL, WIDTHS[1])] = total

    for chunk in range(3):
        z_all(chunk).wait_send()
        x_all(chunk).wait_send()
    for turn_no in range(SWEEPS + 1):
        halo_both(turn_no).wait_send()

    z_all(2).wait_recv()
    table = recv_z[2][...].reshape(rows, WIDTHS[2])
    total = mm(gather_zx, table) + staying[:, STARTS[2] :]
    tail = 729 - SLOT_COL - WIDTHS[1]
    op_ref[:, pl.ds(729 - tail, tail)] = total[:, :tail]
    place = RHS_COL - STARTS[2]
    crhs_ref[...] = total.T[place : place + 27]


def per_device(sizes, start, rhs, diag_block, precond, lift, neighbour, orient, owner, slot):
    nz, nxc, ny = sizes
    rows = nz * nxc * 2
    vmem = pl.BlockSpec(memory_space=pltpu.VMEM)
    anywhere = pl.BlockSpec(memory_space=pl.ANY)
    rmat = jnp.asarray(split_restrict().astype(BF16))
    scratch = [
        pltpu.VMEM((64, 128), F32),
        pltpu.VMEM((64, 128), F32),
        pltpu.VMEM((64, 64, 128), BF16),
        pltpu.VMEM((64, 64, 128), BF16),
        pltpu.VMEM((6, 16, 64), F32),
        pltpu.VMEM((6, 128), jnp.int32),
        pltpu.VMEM((6, 128), jnp.int32),
        pltpu.VMEM((1, 128), jnp.int32),
        pltpu.VMEM((1, 128), jnp.int32),
        pltpu.VMEM((64, 64), BF16),
        pltpu.VMEM((36, 32, 128), F32),
        pltpu.VMEM((COLS, 128), F32),
        pltpu.VMEM((128, 128), F32),
        pltpu.VMEM((128, 128), F32),
        pltpu.VMEM((8, 128), jnp.int32),
        pltpu.VMEM((8, 128), jnp.int32),
        pltpu.VMEM((SWEEPS + 1, 2, 16, 128), F32),
        pltpu.VMEM((SWEEPS + 1, 2, 16, 128), F32),
        pltpu.VMEM((64, 128), F32),
        pltpu.VMEM((rows, 128), BF16),
        pltpu.VMEM((rows, rows), BF16),
        pltpu.VMEM((rows, rows), BF16),
    ]
    for blocks, depth in ((nz, nxc * 2), (nz, nxc * 2), (nxc, nz * 2), (nxc, nz * 2)):
        scratch += [pltpu.VMEM((blocks, depth, width), BF16) for width in WIDTHS]
    scratch += [
        pltpu.SemaphoreType.DMA((13,)),
        pltpu.SemaphoreType.DMA((3,)),
        pltpu.SemaphoreType.DMA((3,)),
        pltpu.SemaphoreType.DMA((3,)),
        pltpu.SemaphoreType.DMA((3,)),
        pltpu.SemaphoreType.DMA((SWEEPS + 1,)),
        pltpu.SemaphoreType.DMA((SWEEPS + 1,)),
        pltpu.SemaphoreType.REGULAR((2,)),
        pltpu.SemaphoreType.REGULAR((2,)),
    ]
    sol, op, crhs = pl.pallas_call(
        functools.partial(kernel, nz, nxc, ny),
        out_shape=(
            jax.ShapeDtypeStruct((64, 128), F32),
            jax.ShapeDtypeStruct((64, 729), F32),
            jax.ShapeDtypeStruct((27, 64), F32),
        ),
        in_specs=[anywhere] * 10,
        out_specs=(vmem, vmem, vmem),
        scratch_shapes=scratch,
        compiler_params=pltpu.CompilerParams(
            collective_id=0, has_side_effects=True, vmem_limit_bytes=60 * 1024 * 1024
        ),
    )(
        start,
        rhs,
        diag_block,
        precond,
        lift,
        neighbour,
        orient,
        owner.reshape(1, -1),
        slot.reshape(1, -1),
        rmat,
    )
    return (sol, op.T, crhs)


def solution(mesh):
    sizes = (mesh.shape["dom"] // 8, 8, mesh.shape["face"])
    return jax.shard_map(
        functools.partial(per_device, sizes),
        mesh=mesh,
        in_specs=(
            P(None, ("dom", "face")),
            P(None, ("dom", "face")),
            P(None, None, ("dom", "face")),
            P(None, None, ("dom", "face")),
            P(),
            P(None, ("dom", "face")),
            P(None, ("dom", "face")),
            P(("dom", "face")),
            P(("dom", "face")),
        ),
        out_specs=(P(None, ("dom", "face")), P(None, ("dom", "face")), P(None, ("dom", "face"))),
        check_vma=False,
    )
```

time: 49.9 us -> 44 us (0.88)
  Pallas kernels: 43.7 us -> 39.6 us
  local copies, waits for them, and re-layouts: 5.22 us -> 3.61 us
    pallas_call x1, Pallas kernels: 43.7 us -> 39.6 us  [per_device(): pl.pallas_call(functools.partial(kernel, nz, nxc, ny), out_shape=(jax.Sha...]
    pad x1 -> x0, local copies, waits for them, and re-layouts: 0.84 us -> none  [per_device(): lift_wide = jnp.pad(lift, ((0, 0), (0, 0), (0, 64)))]
    unnamed x21 -> x5, local copies, waits for them, and re-layouts: 4.37 us -> 3.61 us
where the time goes in v2:
time: 44 us; the launch traced here: 43.8 us
  Pallas kernels  39.6 us (90%)
  local copies, waits for them, and re-layouts  3.61 us (8%)
  between operations  0.64 us (1%)
    pallas_call x1, Pallas kernels, per_device(): pl.pallas_call(functools.partial(kernel, nz, nxc, ny), out_shape=(jax.Sha...  39.6 us
    unnamed x5, local copies, waits for them, and re-layouts  3.61 us

profile of v2, /device:TPU:1, one launch (start us, length us, event | category | flops | bytes accessed | tf_op | source)
XLA Modules:
  0.0 43.8 jit_solution(2083857635490459564)
XLA Ops:
  0.6 39.6 %shard_map.121 = (f32[64,128]{1,0:T(8,128)}, f32[64,729]{1,0:T(8,128)}, f32[27,64]{1,0:T(8,128)}) custom-call(f32[64,128]{1,0:T(8,128)} %start_hbm.1, f32[64,128]{1,0:T(8,128)} %rhs_hbm.1, bf16[64,64,128]{2,1,0:T(8,128)(2,1)} %diag_hbm.1, bf16[64,64,128]{2,1,0:T(8,128)(2,1)} %prec_hbm.1, f32[6,16,64]{2,1,0:T(8,128)} %lift_hbm.1, s32[6,128]{1,0:T(8,128)} %nb_hbm.1, ...), custom_call_target="tpu_custom_call" | custom-call | tf_op jit(solution)/shard_map/pallas_call | solution.py:543
  40.2 1.4 %copy.16 = f32[64,128]{1,0:T(8,128)} copy(f32[64,128]{1,0:T(8,128)} %get-tuple-element.12) | data formatting | bytes 65536
  41.6 0.0 copy-start
  41.6 1.6 %copy.17 = f32[729,64]{0,1:T(8,128)} copy(f32[729,64]{0,1:T(8,128)} %bitcast.3) | data formatting | bytes 373248
  43.2 0.0 copy-done
  43.2 0.6 %copy.18 = f32[27,64]{1,0:T(8,128)} copy(f32[27,64]{1,0:T(8,128)S(1)} %copy-done) | data formatting | bytes 13824
Async XLA Ops:
  41.6 1.6 %copy-start = (f32[27,64]{1,0:T(8,128)S(1)}, f32[27,64]{1,0:T(8,128)}, u32[]{:S(2)}) copy-start(f32[27,64]{1,0:T(8,128)} %get-tuple-element.14) | copy-start | bytes 20740

commit v3 on v2

--- a/solution.py
+++ b/solution.py
@@ -281,9 +281,8 @@
     def columns(chunk):
         return coarse[pl.ds(STARTS[chunk], WIDTHS[chunk]), :].astype(BF16)
 
-    for chunk in (0, 1):
-        packed = nt(pick_z, columns(chunk)).astype(BF16)
-        send_z[chunk][...] = packed.reshape(nz, nxc * 2, WIDTHS[chunk])
+    packed = nt(pick_z, columns(0)).astype(BF16)
+    send_z[0][...] = packed.reshape(nz, nxc * 2, WIDTHS[0])
 
     def z_copy(chunk, shift):
         other = lax.rem(z + shift + nz, nz)
@@ -339,10 +338,20 @@
 
         recv_x[chunk][xc] = send_x[chunk][xc]
 
+    def pack_x(chunk):
+        packed = nt(pick_x[...], columns(chunk)).astype(BF16)
+        send_x[chunk][...] = packed.reshape(nxc, nz * 2, WIDTHS[chunk])
+        start_x(chunk)
+
     half = nz // 2
-    for chunk in (0, 1):
-        for shift in range(1, min(2, half) + 1):
-            z_pair(chunk, shift)
+    for shift in range(1, min(2, half) + 1):
+        z_pair(0, shift)
+    s = lax.broadcasted_iota(jnp.int32, (rows, 128), 0)
+    deep = 2 * nz
+    wide = 2 * nxc
+    target = (((s & (deep - 1)) >> 1) * wide) + ((s // deep) * 2) + (s & 1)
+    pick_x[...] = one_hot(target == key)
+    pack_x(1)
     if nz > 4:
         for side in range(2):
             pl.semaphore_wait(near_sem.at[side], 1)
@@ -351,10 +360,22 @@
                 pl.semaphore_signal(
                     far_sem.at[side], inc=1, device_id=at_z(shift), device_id_type=MESH
                 )
-        for chunk in (0, 1):
-            for shift in range(3, min(4, half) + 1):
-                z_pair(chunk, shift)
-    for chunk in (0, 1):
+        for shift in range(3, min(4, half) + 1):
+            z_pair(0, shift)
+    recv_z[0][z] = send_z[0][z]
+
+    s = lax.broadcasted_iota(jnp.int32, (rows, rows), 0)
+    q = lax.broadcasted_iota(jnp.int32, (rows, rows), 1)
+    target = (((s & (deep - 1)) >> 1) * wide) + ((s // deep) * 2) + (s & 1)
+    move_zx[...] = one_hot(q == target)
+    target = (((s & (wide - 1)) >> 1) * deep) + ((s // wide) * 2) + (s & 1)
+    move_xz[...] = one_hot(q == target)
+
+    def onward(chunk):
+        x_all(chunk).wait_recv()
+        table = recv_x[chunk][...].reshape(rows, WIDTHS[chunk])
+        moved = mm(move_xz[...], table).astype(BF16)
+        send_z[chunk][...] = moved.reshape(nz, nxc * 2, WIDTHS[chunk])
         recv_z[chunk][z] = send_z[chunk][z]
 
     for fetch in fetches[4:7]:
@@ -424,50 +445,33 @@
             if nz > 8:
                 for side in range(2):
                     pl.semaphore_wait(far_sem.at[side], 1)
-                for chunk in (0, 1):
-                    for shift in range(half, 4, -1):
-                        z_pair(chunk, shift)
-            s = lax.broadcasted_iota(jnp.int32, (rows, 128), 0)
-            deep = 2 * nz
-            wide = 2 * nxc
-            target = (((s & (deep - 1)) >> 1) * wide) + ((s // deep) * 2) + (s & 1)
-            pick_x[...] = one_hot(target == key)
-            s = lax.broadcasted_iota(jnp.int32, (rows, rows), 0)
-            q = lax.broadcasted_iota(jnp.int32, (rows, rows), 1)
-            target = (((s & (deep - 1)) >> 1) * wide) + ((s // deep) * 2) + (s & 1)
-            move_zx[...] = one_hot(q == target)
-            target = (((s & (wide - 1)) >> 1) * deep) + ((s // wide) * 2) + (s & 1)
-            move_xz[...] = one_hot(q == target)
+                for shift in range(half, 4, -1):
+                    z_pair(0, shift)
+            onward(1)
+            for shift in range(half, 0, -1):
+                z_pair(1, shift)
     sol_ref[...] = val[...]
     through = rhs_ref[...] - matvec(diag_ref, val[...])
     resid = through + coupled(SWEEPS)
     both = mm(rmat, resid.astype(BF16))
     coarse[pl.ds(RHS_COL, 32), :] = both[:32] + both[32:]
-    packed = nt(pick_x[...], columns(2)).astype(BF16)
-    send_x[2][...] = packed.reshape(nxc, nz * 2, WIDTHS[2])
-    start_x(2)
-
-    def forward(chunk):
-        z_all(chunk).wait_recv()
-        table = recv_z[chunk][...].reshape(rows, WIDTHS[chunk])
-        moved = mm(move_zx[...], table).astype(BF16)
-        send_x[chunk][...] = moved.reshape(nxc, nz * 2, WIDTHS[chunk])
-        start_x(chunk)
-
-    forward(0)
+    pack_x(2)
+
+    z_all(0).wait_recv()
+    table = recv_z[0][...].reshape(rows, WIDTHS[0])
+    moved = mm(move_zx[...], table).astype(BF16)
+    send_x[0][...] = moved.reshape(nxc, nz * 2, WIDTHS[0])
+    start_x(0)
+
     agg_rows = lax.broadcasted_iota(jnp.int32, (64, 128), 0)
     stay = one_hot((agg_rows == slot_ref[...]) & (lane < 32))
     stay_hi, stay_lo = halves(coarse[...])
     staying = nt(stay, stay_hi) + nt(stay, stay_lo)
 
-    x_all(2).wait_recv()
-    moved = mm(move_xz[...], recv_x[2][...].reshape(rows, WIDTHS[2])).astype(BF16)
-    send_z[2][...] = moved.reshape(nz, nxc * 2, WIDTHS[2])
+    onward(2)
     for shift in range(half, 0, -1):
         z_pair(2, shift)
-    recv_z[2][z] = send_z[2][z]
-
-    forward(1)
+
     x_all(0).wait_recv()
     table = recv_x[0][...].reshape(rows, WIDTHS[0])
     want = lax.broadcasted_iota(jnp.int32, (8, WIDTHS[0]), 1) == SLOT_COL
@@ -477,9 +481,9 @@
     gather_zx = mm(gather, move_zx[...]).astype(BF16)
     total = mm(gather, table) + staying[:, : WIDTHS[0]]
     op_ref[:, pl.ds(0, SLOT_COL)] = total[:, :SLOT_COL]
-    x_all(1).wait_recv()
-    table = recv_x[1][...].reshape(rows, WIDTHS[1])
-    total = mm(gather, table) + staying[:, STARTS[1] : STARTS[2]]
+    z_all(1).wait_recv()
+    table = recv_z[1][...].reshape(rows, WIDTHS[1])
+    total = mm(gather_zx, table) + staying[:, STARTS[1] : STARTS[2]]
     op_ref[:, pl.ds(SLOT_COL, WIDTHS[1])] = total
 
     for chunk in range(3):
@@ -497,11 +501,17 @@
     crhs_ref[...] = total.T[place : place + 27]
 
 
+def hand_over(sol_in, op_in, crhs_in, sol_ref, op_ref, crhs_ref):
+    sol_ref[...] = sol_in[...]
+    op_ref[...] = op_in[...]
+    crhs_ref[...] = crhs_in[...]
+
+
 def per_device(sizes, start, rhs, diag_block, precond, lift, neighbour, orient, owner, slot):
     nz, nxc, ny = sizes
     rows = nz * nxc * 2
     vmem = pl.BlockSpec(memory_space=pltpu.VMEM)
-    anywhere = pl.BlockSpec(memory_space=pl.ANY)
+    anywhere = pl.BlockSpec(memory_space=pltpu.HBM)
     rmat = jnp.asarray(split_restrict().astype(BF16))
     scratch = [
         pltpu.VMEM((64, 128), F32),
@@ -540,7 +550,7 @@
         pltpu.SemaphoreType.REGULAR((2,)),
         pltpu.SemaphoreType.REGULAR((2,)),
     ]
-    sol, op, crhs = pl.pallas_call(
+    parts = pl.pallas_call(
         functools.partial(kernel, nz, nxc, ny),
         out_shape=(
             jax.ShapeDtypeStruct((64, 128), F32),
@@ -565,6 +575,12 @@
         slot.reshape(1, -1),
         rmat,
     )
+    sol, op, crhs = pl.pallas_call(
+        hand_over,
+        out_shape=tuple(jax.ShapeDtypeStruct(part.shape, F32) for part in parts),
+        in_specs=[vmem] * 3,
+        out_specs=(vmem, vmem, vmem),
+    )(*parts)
     return (sol, op.T, crhs)
 
 

time: 44 us -> 41.1 us (0.934)
  the two profiles are of different devices: /device:TPU:1 before, /device:TPU:24 now
where the time goes in v3:
time: 41.1 us; the launch traced here: 41 us
  Pallas kernels  40.4 us (98%)
  between operations  0.64 us (2%)
    pallas_call x1, Pallas kernels, per_device(): pl.pallas_call(functools.partial(kernel, nz, nxc, ny), out_shape=(jax.Sha...  38.7 us
    pallas_call x1, Pallas kernels, per_device(): pl.pallas_call(hand_over, out_shape=tuple((jax.ShapeDtypeStruct(part.shap...  1.62 us

profile of v3, /device:TPU:24, one launch (start us, length us, event | category | flops | bytes accessed | tf_op | source)
XLA Modules:
  0.0 41.0 jit_solution(5706180818626403016)
XLA Ops:
  0.6 38.7 %shard_map.121 = (f32[64,128]{1,0:T(8,128)}, f32[64,729]{1,0:T(8,128)}, f32[27,64]{1,0:T(8,128)}) custom-call(f32[64,128]{1,0:T(8,128)} %start_hbm.1, f32[64,128]{1,0:T(8,128)} %rhs_hbm.1, bf16[64,64,128]{2,1,0:T(8,128)(2,1)} %diag_hbm.1, bf16[64,64,128]{2,1,0:T(8,128)(2,1)} %prec_hbm.1, f32[6,16,64]{2,1,0:T(8,128)} %lift_hbm.1, s32[6,128]{1,0:T(8,128)} %nb_hbm.1, ...), custom_call_target="tpu_custom_call" | custom-call | tf_op jit(solution)/shard_map/pallas_call | solution.py:553
  39.4 1.6 %shard_map.122 = (f32[64,128]{1,0:T(8,128)}, f32[64,729]{1,0:T(8,128)}, f32[27,64]{1,0:T(8,128)}) custom-call(f32[64,128]{1,0:T(8,128)} %get-tuple-element.9.sol_in, f32[64,729]{1,0:T(8,128)} %get-tuple-element.10.op_in, f32[27,64]{1,0:T(8,128)} %get-tuple-element.11.crhs_in), custom_call_target="tpu_custom_call" | custom-call | tf_op jit(solution)/shard_map/pallas_call | solution.py:578

commit v4 on v3

--- a/solution.py
+++ b/solution.py
@@ -10,10 +10,10 @@
 
 SWEEPS = 2
 MESH = pl.DeviceIdType.MESH
-WIDTHS = (384, 256, 128)
-STARTS = (0, 384, 640)
+WIDTHS = (256, 384, 128)
+STARTS = (0, 256, 640)
 COLS = 768
-SLOT_COL = 383
+SLOT_COL = 255
 RHS_COL = 736
 F32 = jnp.float32
 BF16 = jnp.bfloat16
@@ -203,21 +203,32 @@
         return pltpu.make_async_remote_copy(
             src_ref=halo_out.at[turn_no, side],
             dst_ref=halo_in.at[turn_no, side],
-            send_sem=hs_sem.at[turn_no],
-            recv_sem=hr_sem.at[turn_no],
+            send_sem=hs_sem.at[turn_no, side],
+            recv_sem=hr_sem.at[turn_no, side],
             device_id=(dom, above if side == 0 else below),
             device_id_type=MESH,
         )
 
-    def halo_both(turn_no):
-        return pltpu.make_async_remote_copy(
-            src_ref=halo_out.at[turn_no],
-            dst_ref=halo_in.at[turn_no],
-            send_sem=hs_sem.at[turn_no],
-            recv_sem=hr_sem.at[turn_no],
-            device_id=(dom, above),
-            device_id_type=MESH,
-        )
+    sends_to = (y < ny - 1, y > 0)
+    gets_from = (y > 0, y < ny - 1)
+
+    def halo_start(turn_no):
+        for side in range(2):
+            @pl.when(sends_to[side])
+            def _():
+                halo_copy(turn_no, side).start()
+
+    def halo_wait(turn_no):
+        for side in range(2):
+            @pl.when(gets_from[side])
+            def _():
+                halo_copy(turn_no, side).wait_recv()
+
+    def halo_sent(turn_no):
+        for side in range(2):
+            @pl.when(sends_to[side])
+            def _():
+                halo_copy(turn_no, side).wait_send()
 
     def send_halo(turn_no):
         low = jnp.concatenate([val[pl.ds(16 * i, 4), :] for i in range(4)], 0)
@@ -229,8 +240,7 @@
     send_halo(0)
 
     pl.semaphore_wait(barrier, 2 + 4 + nxc - 1)
-    for side in range(2):
-        halo_copy(0, side).start()
+    halo_start(0)
     if nz > 4:
         for side, shift in enumerate((2, -2)):
             pl.semaphore_signal(
@@ -420,7 +430,7 @@
             )
             for k in range(16)
         ]
-        halo_both(turn_no).wait_recv()
+        halo_wait(turn_no)
         low = jnp.where(y > 0, halo_in[turn_no, 0], 0.0)
         high = jnp.where(y < ny - 1, halo_in[turn_no, 1], 0.0)
         cells = [jnp.where(from_low, low[k : k + 1], cells[k]) for k in range(16)]
@@ -431,22 +441,29 @@
         turned_hi, turned_lo = halves(jnp.concatenate(cells, 0))
         return mm(lift_hi, turned_hi) + (mm(lift_hi, turned_lo) + mm(lift_lo, turned_hi))
 
+    def smooth(places, resid):
+        for place in places:
+            part = prec_ref[pl.ds(place, 4)].astype(F32) * resid[None]
+            val[pl.ds(place, 4), :] = val[pl.ds(place, 4), :] + jnp.sum(part, axis=1)
+
+    edges = [16 * i + j for i in range(4) for j in (0, 12)]
+    inner = [16 * i + j for i in range(4) for j in (4, 8)]
+    if nz > 8:
+        for side in range(2):
+            pl.semaphore_wait(far_sem.at[side], 1)
+        for shift in range(half, 4, -1):
+            z_pair(0, shift)
     fetches[7].wait()
     for sweep in range(SWEEPS):
         through = rhs_ref[...] - matvec(diag_ref, val[...])
         resid = through + coupled(sweep)
         if sweep == 0:
             fetches[8].wait()
-        val[...] = val[...] + matvec(prec_ref, resid)
+        smooth(edges, resid)
         send_halo(sweep + 1)
-        for side in range(2):
-            halo_copy(sweep + 1, side).start()
+        halo_start(sweep + 1)
+        smooth(inner, resid)
         if sweep == 0:
-            if nz > 8:
-                for side in range(2):
-                    pl.semaphore_wait(far_sem.at[side], 1)
-                for shift in range(half, 4, -1):
-                    z_pair(0, shift)
             onward(1)
             for shift in range(half, 0, -1):
                 z_pair(1, shift)
@@ -457,20 +474,20 @@
     coarse[pl.ds(RHS_COL, 32), :] = both[:32] + both[32:]
     pack_x(2)
 
+    agg_rows = lax.broadcasted_iota(jnp.int32, (64, 128), 0)
+    stay = one_hot((agg_rows == slot_ref[...]) & (lane < 32))
+    stay_hi, stay_lo = halves(coarse[...])
+    staying = nt(stay, stay_hi) + nt(stay, stay_lo)
+
+    onward(2)
+    for shift in range(half, 0, -1):
+        z_pair(2, shift)
+
     z_all(0).wait_recv()
     table = recv_z[0][...].reshape(rows, WIDTHS[0])
     moved = mm(move_zx[...], table).astype(BF16)
     send_x[0][...] = moved.reshape(nxc, nz * 2, WIDTHS[0])
     start_x(0)
-
-    agg_rows = lax.broadcasted_iota(jnp.int32, (64, 128), 0)
-    stay = one_hot((agg_rows == slot_ref[...]) & (lane < 32))
-    stay_hi, stay_lo = halves(coarse[...])
-    staying = nt(stay, stay_hi) + nt(stay, stay_lo)
-
-    onward(2)
-    for shift in range(half, 0, -1):
-        z_pair(2, shift)
 
     x_all(0).wait_recv()
     table = recv_x[0][...].reshape(rows, WIDTHS[0])
@@ -490,7 +507,7 @@
         z_all(chunk).wait_send()
         x_all(chunk).wait_send()
     for turn_no in range(SWEEPS + 1):
-        halo_both(turn_no).wait_send()
+        halo_sent(turn_no)
 
     z_all(2).wait_recv()
     table = recv_z[2][...].reshape(rows, WIDTHS[2])
@@ -545,8 +562,8 @@
         pltpu.SemaphoreType.DMA((3,)),
         pltpu.SemaphoreType.DMA((3,)),
         pltpu.SemaphoreType.DMA((3,)),
-        pltpu.SemaphoreType.DMA((SWEEPS + 1,)),
-        pltpu.SemaphoreType.DMA((SWEEPS + 1,)),
+        pltpu.SemaphoreType.DMA((SWEEPS + 1, 2)),
+        pltpu.SemaphoreType.DMA((SWEEPS + 1, 2)),
         pltpu.SemaphoreType.REGULAR((2,)),
         pltpu.SemaphoreType.REGULAR((2,)),
     ]

time: 41.1 us -> 40.1 us (0.976)
  the two profiles are of different devices: /device:TPU:24 before, /device:TPU:1 now
where the time goes in v4:
time: 40.1 us; the launch traced here: 40 us
  Pallas kernels  39.3 us (98%)
  between operations  0.64 us (2%)
    pallas_call x1, Pallas kernels, per_device(): pl.pallas_call(functools.partial(kernel, nz, nxc, ny), out_shape=(jax.Sha...  37.7 us
    pallas_call x1, Pallas kernels, per_device(): pl.pallas_call(hand_over, out_shape=tuple((jax.ShapeDtypeStruct(part.shap...  1.62 us

profile of v4, /device:TPU:1, one launch (start us, length us, event | category | flops | bytes accessed | tf_op | source)
XLA Modules:
  0.0 40.0 jit_solution(16494134230429440174)
XLA Ops:
  0.6 37.7 %shard_map.121 = (f32[64,128]{1,0:T(8,128)}, f32[64,729]{1,0:T(8,128)}, f32[27,64]{1,0:T(8,128)}) custom-call(f32[64,128]{1,0:T(8,128)} %start_hbm.1, f32[64,128]{1,0:T(8,128)} %rhs_hbm.1, bf16[64,64,128]{2,1,0:T(8,128)(2,1)} %diag_hbm.1, bf16[64,64,128]{2,1,0:T(8,128)(2,1)} %prec_hbm.1, f32[6,16,64]{2,1,0:T(8,128)} %lift_hbm.1, s32[6,128]{1,0:T(8,128)} %nb_hbm.1, ...), custom_call_target="tpu_custom_call" | custom-call | tf_op jit(solution)/shard_map/pallas_call | solution.py:570
  38.3 1.6 %shard_map.122 = (f32[64,128]{1,0:T(8,128)}, f32[64,729]{1,0:T(8,128)}, f32[27,64]{1,0:T(8,128)}) custom-call(f32[64,128]{1,0:T(8,128)} %get-tuple-element.9.sol_in, f32[64,729]{1,0:T(8,128)} %get-tuple-element.10.op_in, f32[27,64]{1,0:T(8,128)} %get-tuple-element.11.crhs_in), custom_call_target="tpu_custom_call" | custom-call | tf_op jit(solution)/shard_map/pallas_call | solution.py:595

commit v5 on v4

--- a/solution.py
+++ b/solution.py
@@ -140,7 +140,6 @@
     xr_sem,
     hs_sem,
     hr_sem,
-    near_sem,
     far_sem,
 ):
     send_z = (send_z0, send_z1, send_z2)
@@ -161,7 +160,7 @@
     barrier = pltpu.get_barrier_semaphore()
     for other in (above, below):
         pl.semaphore_signal(barrier, inc=1, device_id=(dom, other), device_id_type=MESH)
-    for shift in (1, -1, 2, -2):
+    for shift in (1, -1, 2, -2, 3, -3, 4, -4):
         pl.semaphore_signal(barrier, inc=1, device_id=at_z(shift), device_id_type=MESH)
 
     @pl.loop(1, nxc)
@@ -239,12 +238,12 @@
     fetches[0].wait()
     send_halo(0)
 
-    pl.semaphore_wait(barrier, 2 + 4 + nxc - 1)
+    pl.semaphore_wait(barrier, 2 + 8 + nxc - 1)
     halo_start(0)
-    if nz > 4:
-        for side, shift in enumerate((2, -2)):
+    if nz > 8:
+        for side, shift in enumerate((4, -4)):
             pl.semaphore_signal(
-                near_sem.at[side], inc=1, device_id=at_z(shift), device_id_type=MESH
+                far_sem.at[side], inc=1, device_id=at_z(shift), device_id_type=MESH
             )
 
     coarse[pl.ds(728, 40), :] = jnp.zeros((40, 128), F32)
@@ -363,13 +362,6 @@
     pick_x[...] = one_hot(target == key)
     pack_x(1)
     if nz > 4:
-        for side in range(2):
-            pl.semaphore_wait(near_sem.at[side], 1)
-        if nz > 8:
-            for side, shift in enumerate((4, -4)):
-                pl.semaphore_signal(
-                    far_sem.at[side], inc=1, device_id=at_z(shift), device_id_type=MESH
-                )
         for shift in range(3, min(4, half) + 1):
             z_pair(0, shift)
     recv_z[0][z] = send_z[0][z]
@@ -416,7 +408,7 @@
             product[pl.ds(8 * block, 8), :] = jnp.sum(part, axis=1)
         return product[...]
 
-    def coupled(turn_no):
+    def coupled(turn_no, meanwhile):
         trace[pl.ds(1, 16, stride=8), :] = val[pl.ds(0, 16), :]
         trace[pl.ds(0, 16, stride=8), :] = val[pl.ds(48, 16), :]
         for i in range(4):
@@ -430,6 +422,7 @@
             )
             for k in range(16)
         ]
+        meanwhile()
         halo_wait(turn_no)
         low = jnp.where(y > 0, halo_in[turn_no, 0], 0.0)
         high = jnp.where(y < ny - 1, halo_in[turn_no, 1], 0.0)
@@ -448,15 +441,21 @@
 
     edges = [16 * i + j for i in range(4) for j in (0, 12)]
     inner = [16 * i + j for i in range(4) for j in (4, 8)]
-    if nz > 8:
-        for side in range(2):
-            pl.semaphore_wait(far_sem.at[side], 1)
-        for shift in range(half, 4, -1):
-            z_pair(0, shift)
+    def far_sends():
+        if nz > 8:
+            for side in range(2):
+                pl.semaphore_wait(far_sem.at[side], 1)
+            for shift in range(half, 4, -1):
+                z_pair(0, shift)
+
+    def nothing():
+        pass
+
+    hooks = (far_sends, nothing, nothing)
     fetches[7].wait()
     for sweep in range(SWEEPS):
         through = rhs_ref[...] - matvec(diag_ref, val[...])
-        resid = through + coupled(sweep)
+        resid = through + coupled(sweep, hooks[sweep])
         if sweep == 0:
             fetches[8].wait()
         smooth(edges, resid)
@@ -469,7 +468,7 @@
                 z_pair(1, shift)
     sol_ref[...] = val[...]
     through = rhs_ref[...] - matvec(diag_ref, val[...])
-    resid = through + coupled(SWEEPS)
+    resid = through + coupled(SWEEPS, hooks[SWEEPS])
     both = mm(rmat, resid.astype(BF16))
     coarse[pl.ds(RHS_COL, 32), :] = both[:32] + both[32:]
     pack_x(2)
@@ -565,7 +564,6 @@
         pltpu.SemaphoreType.DMA((SWEEPS + 1, 2)),
         pltpu.SemaphoreType.DMA((SWEEPS + 1, 2)),
         pltpu.SemaphoreType.REGULAR((2,)),
-        pltpu.SemaphoreType.REGULAR((2,)),
     ]
     parts = pl.pallas_call(
         functools.partial(kernel, nz, nxc, ny),

time: 40.1 us -> 39 us (0.973)
  Pallas kernels: 39.3 us -> 38.2 us
    pallas_call x1, Pallas kernels: 37.7 us -> 36.6 us  [per_device(): pl.pallas_call(functools.partial(kernel, nz, nxc, ny), out_shape=(jax.Sha...]
where the time goes in v5:
time: 39 us; the launch traced here: 38.9 us
  Pallas kernels  38.2 us (98%)
  between operations  0.64 us (2%)
    pallas_call x1, Pallas kernels, per_device(): pl.pallas_call(functools.partial(kernel, nz, nxc, ny), out_shape=(jax.Sha...  36.6 us
    pallas_call x1, Pallas kernels, per_device(): pl.pallas_call(hand_over, out_shape=tuple((jax.ShapeDtypeStruct(part.shap...  1.62 us

profile of v5, /device:TPU:1, one launch (start us, length us, event | category | flops | bytes accessed | tf_op | source)
XLA Modules:
  0.0 38.9 jit_solution(12147390555861739271)
XLA Ops:
  0.6 36.6 %shard_map.121 = (f32[64,128]{1,0:T(8,128)}, f32[64,729]{1,0:T(8,128)}, f32[27,64]{1,0:T(8,128)}) custom-call(f32[64,128]{1,0:T(8,128)} %start_hbm.1, f32[64,128]{1,0:T(8,128)} %rhs_hbm.1, bf16[64,64,128]{2,1,0:T(8,128)(2,1)} %diag_hbm.1, bf16[64,64,128]{2,1,0:T(8,128)(2,1)} %prec_hbm.1, f32[6,16,64]{2,1,0:T(8,128)} %lift_hbm.1, s32[6,128]{1,0:T(8,128)} %nb_hbm.1, ...), custom_call_target="tpu_custom_call" | custom-call | tf_op jit(solution)/shard_map/pallas_call | solution.py:568
  37.2 1.6 %shard_map.122 = (f32[64,128]{1,0:T(8,128)}, f32[64,729]{1,0:T(8,128)}, f32[27,64]{1,0:T(8,128)}) custom-call(f32[64,128]{1,0:T(8,128)} %get-tuple-element.9.sol_in, f32[64,729]{1,0:T(8,128)} %get-tuple-element.10.op_in, f32[27,64]{1,0:T(8,128)} %get-tuple-element.11.crhs_in), custom_call_target="tpu_custom_call" | custom-call | tf_op jit(solution)/shard_map/pallas_call | solution.py:593
